TPU v7x, 768 devices: a whole 4x8x12 slice. The times are simulated.
768 devices in a mesh: rows: 64 (over y, x, core), cols: 12 (over z).
Axes of the slice: x: 4, y: 8, z: 12, core: 2. Of those that a mesh axis runs over, the one named last changes fastest.
Arguments:
- known_inverse: bfloat16 [12, 64, 32, 24576], P(None, 'rows', None, 'cols'), may hold values from -6 to 6
- lower_panel: bfloat16 [4, 12, 64, 32, 512], P(None, 'cols'), may hold values from -0.0390625 to 0.0390625
- chain_panel: bfloat16 [4, 512, 512], replicated, may hold values from -0.25 to 0.25
- diag_inverse: float32 [4, 512, 512], P(None, 'rows'), may hold values from -6 to 6
- top_cols: bfloat16 [12, 64, 32, 512], P('cols', 'rows'), may hold values from -6 to 6
- top_diag: float32 [512, 512], P('rows'), may hold values from -6 to 6
- pattern: int32 [4, 768], replicated, may hold values from 0 to 1, as said below
Outputs:
- inverse_cols: bfloat16 [4, 12, 64, 32, 512], P(None, 'cols', 'rows')
- inverse_diag: float32 [4, 512, 512], P(None, 'rows')
- inverse_sub: float32 [4, 512, 512], P(None, 'rows')
Inputs may be any that keep to these rules, and one draw needn't show every extreme that they name: `pattern`: row k marks exactly (768 * (5 + k)) // 9 block rows, and every block row marked in row k is marked in row k + 1.
All inputs are finite; a program needn't handle non-finite values.
Results may differ from a plain program's by a relative error of at most 0.025.
Values may be sent and summed in bfloat16 or wider, within the bound.
A program may use at most 128 MiB of HBM per device.

v0:
```python
import jax
import jax.numpy as jnp
from jax import lax
from jax.sharding import PartitionSpec as P


def local(known_inverse, lower_panel, chain_panel, diag_inverse, top_cols, top_diag, pattern):
    n_rows = lax.axis_size("rows")
    n_cols = lax.axis_size("cols")
    row_id = lax.axis_index("rows")
    col_id = lax.axis_index("cols")
    supers = lower_panel.shape[0]
    piece_rows = known_inverse.shape[2]
    panel_width = lower_panel.shape[-1]
    diag_count = panel_width // n_rows
    known_rows = known_inverse.reshape(n_cols * piece_rows, -1)
    group_mask = lax.dynamic_slice_in_dim(pattern, col_id * n_rows, n_rows, 1)
    panels = lower_panel[:, 0] * group_mask[:, :, None, None].astype(jnp.bfloat16)
    panel_slab = panels.reshape(supers, n_rows * piece_rows, panel_width)
    own_pieces = lax.dynamic_index_in_dim(panels, row_id, 1, keepdims=False)
    own_mask = lax.dynamic_index_in_dim(group_mask, row_id, 1, keepdims=False).astype(jnp.float32)
    first_col = jnp.where(col_id == 0, 1.0, 0.0).astype(jnp.float32)
    prev_cols = top_cols.reshape(piece_rows, panel_width)
    prev_diag = top_diag
    cols_list = [None] * supers
    diag_list = [None] * supers
    sub_list = [None] * supers
    for section in reversed(range(supers)):
        link_block = chain_panel[section]
        link_wide = link_block.astype(jnp.float32)
        own_panel = own_pieces[section]
        link_rows = lax.dynamic_slice_in_dim(link_wide, row_id * diag_count, diag_count, 0)
        diag_link = jnp.dot(prev_diag, link_wide, precision=lax.Precision.HIGHEST)
        carried = jnp.dot(prev_cols, link_block, preferred_element_type=jnp.float32)
        sub_term = -jnp.einsum(
            "pi,pj->ij", prev_cols, own_panel, preferred_element_type=jnp.float32
        )
        product = lax.psum_scatter(
            jnp.dot(known_rows, panel_slab[section], preferred_element_type=jnp.float32).astype(
                jnp.bfloat16
            ),
            "cols",
            scatter_dimension=0,
            tiled=True,
        ).astype(jnp.float32)
        new_cols = (-(product + carried) * own_mask[section]).astype(jnp.bfloat16)
        diag_term = (
            -jnp.einsum("pi,pj->ij", own_panel, new_cols, preferred_element_type=jnp.float32)
            + jnp.einsum(
                "pi,pj->ij", carried, own_panel.astype(jnp.float32), precision=lax.Precision.HIGHEST
            )
            + first_col
            * jnp.einsum("mi,mj->ij", link_rows, diag_link, precision=lax.Precision.HIGHEST)
        )
        joined = jnp.stack([sub_term, diag_term], axis=1)
        reduced = lax.psum_scatter(joined, "rows", scatter_dimension=0, tiled=True)
        reduced = lax.psum(reduced.astype(jnp.bfloat16), "cols").astype(jnp.float32)
        sub_sum = reduced[:, 0]
        diag_sum = reduced[:, 1]
        sub_block = sub_sum - diag_link
        diag_block = diag_inverse[section] + diag_sum
        cols_list[section] = new_cols
        diag_list[section] = diag_block
        sub_list[section] = sub_block
        prev_cols = new_cols
        prev_diag = diag_block
    cols_out = jnp.stack(cols_list).reshape(supers, 1, 1, piece_rows, panel_width)
    return (cols_out, jnp.stack(diag_list), jnp.stack(sub_list))


def solution(mesh):
    in_specs = (
        P(None, "rows", None, "cols"),
        P(None, "cols", None, None, None),
        P(),
        P(None, "rows", None),
        P("cols", "rows", None, None),
        P("rows", None),
        P(),
    )
    out_specs = (P(None, "cols", "rows", None, None), P(None, "rows", None), P(None, "rows", None))
    return jax.shard_map(local, mesh=mesh, in_specs=in_specs, out_specs=out_specs, check_vma=False)
```

profile of v0, /device:TPU:1, one launch (start us, length us, event | category | flops | bytes accessed | tf_op | source)
XLA Modules:
  0.0 982.0 jit_solution(6020972830035621036)
XLA Ops:
  8.1 7.2 bitcast_multiply_fusion
  15.3 5.7 fusion.83
  21.0 1.3 fusion.15
  22.3 1.0 copy.29
  23.3 2.9 fusion.14
  28.6 2.7 fusion.84
  31.3 1.3 fusion.28
  32.7 1.1 fusion.8
  33.8 46.3 %reduce-scatter.31.cloned.1.call-done = bf16[32,512]{1,0:T(8,128)(2,1)} async-done(((bf16[384,512]{1,0:T(8,128)(2,1)}), bf16[32,512]{1,0:T(8,128)(2,1)}) %reduce-scatter.31.cloned.1.call-update) | async-done | bytes 32784 | tf_op jit(solution)/shard_map/reduce_scatter | solution.py:38
  80.1 1.9 multiply_convert_fusion.3
  82.0 1.1 convolution_negate_fusion
  83.1 1.4 convolution_add_fusion
  84.5 1.4 fusion.7
  85.8 1.6 pad_maximum_fusion
  87.5 2.9 fusion.13
  91.4 1.1 fusion.9
  92.5 45.9 %reduce-scatter.29.cloned.1.call-done = bf16[32,512]{1,0:T(8,128)(2,1)} async-done(((bf16[384,512]{1,0:T(8,128)(2,1)}), bf16[32,512]{1,0:T(8,128)(2,1)}) %reduce-scatter.29.cloned.1.call-update) | async-done | bytes 32784 | tf_op jit(solution)/shard_map/reduce_scatter | solution.py:38
  138.4 1.9 multiply_convert_fusion.2
  140.2 1.1 convolution_negate_fusion.2
  141.3 2.4 convolution_add_fusion.1
  143.7 157.5 %reduce-scatter.17.cloned.1.call-done = f32[8,2,512]{2,0,1:T(8,128)} async-done(((f32[512,2,512]{2,0,1:T(8,128)}), f32[8,2,512]{2,0,1:T(8,128)}) %reduce-scatter.17.cloned.1.call-update) | async-done | bytes 32784 | tf_op jit(solution)/shard_map/reduce_scatter | solution.py:56
  301.9 34.6 %psum.28 = bf16[8,2,512]{2,0,1:T(8,128)(2,1)S(1)} all-reduce(bf16[8,2,512]{2,0,1:T(8,128)(2,1)S(1)} %convert_element_type.106), channel_id=1, replica_groups=mesh['rows'=64,'cols'=12] {'cols'}, use_global_device_ids=true, to_apply=%region_5.6 | all-reduce | flops 8192 | bytes 32768 | tf_op jit(solution)/shard_map/psum | solution.py:57
  336.6 1.3 fusion.24
  337.9 1.9 fusion.5
  339.8 1.6 pad_maximum_fusion.1
  341.5 2.9 fusion.12
  344.4 1.0 copy.23
  345.7 1.1 fusion.10
  346.8 10.6 %reduce-scatter.27.cloned.1.call-done = bf16[32,512]{1,0:T(8,128)(2,1)} async-done(((bf16[384,512]{1,0:T(8,128)(2,1)}), bf16[32,512]{1,0:T(8,128)(2,1)}) %reduce-scatter.27.cloned.1.call-update) | async-done | bytes 32784 | tf_op jit(solution)/shard_map/reduce_scatter | solution.py:38
  357.4 1.9 multiply_convert_fusion.1
  359.3 1.1 convolution_negate_fusion.4
  360.4 2.5 convolution_add_fusion.2
  362.8 157.3 %reduce-scatter.19.cloned.1.call-done = f32[8,2,512]{2,0,1:T(8,128)} async-done(((f32[512,2,512]{2,0,1:T(8,128)}), f32[8,2,512]{2,0,1:T(8,128)}) %reduce-scatter.19.cloned.1.call-update) | async-done | bytes 32784 | tf_op jit(solution)/shard_map/reduce_scatter | solution.py:56
  520.9 34.8 %psum.29 = bf16[8,2,512]{2,0,1:T(8,128)(2,1)S(1)} all-reduce(bf16[8,2,512]{2,0,1:T(8,128)(2,1)S(1)} %convert_element_type.108), channel_id=1, replica_groups=mesh['rows'=64,'cols'=12] {'cols'}, use_global_device_ids=true, to_apply=%region_7.8 | all-reduce | flops 8192 | bytes 32768 | tf_op jit(solution)/shard_map/psum | solution.py:57
  555.7 1.3 fusion.20
  557.0 1.9 fusion.3
  558.9 1.6 pad_maximum_fusion.2
  560.6 2.1 fusion.11
  562.7 13.4 %reduce-scatter.25.cloned.1.call-done = bf16[32,512]{1,0:T(8,128)(2,1)} async-done(((bf16[384,512]{1,0:T(8,128)(2,1)}), bf16[32,512]{1,0:T(8,128)(2,1)}) %reduce-scatter.25.cloned.1.call-update) | async-done | bytes 32784 | tf_op jit(solution)/shard_map/reduce_scatter | solution.py:38
  576.1 1.9 multiply_convert_fusion
  578.0 1.1 convolution_negate_fusion.6
  579.1 1.4 convolution_add_fusion.3
  580.5 158.8 %reduce-scatter.21.cloned.1.call-done = f32[8,2,512]{2,0,1:T(8,128)} async-done(((f32[512,2,512]{2,0,1:T(8,128)}), f32[8,2,512]{2,0,1:T(8,128)}) %reduce-scatter.21.cloned.1.call-update) | async-done | bytes 32784 | tf_op jit(solution)/shard_map/reduce_scatter | solution.py:56
  740.0 34.2 %psum.30 = bf16[8,2,512]{2,0,1:T(8,128)(2,1)S(1)} all-reduce(bf16[8,2,512]{2,0,1:T(8,128)(2,1)S(1)} %convert_element_type.110), channel_id=1, replica_groups=mesh['rows'=64,'cols'=12] {'cols'}, use_global_device_ids=true, to_apply=%region_9.10 | all-reduce | flops 8192 | bytes 32768 | tf_op jit(solution)/shard_map/psum | solution.py:57
  774.2 1.4 fusion.16
  776.4 1.5 pad_maximum_fusion.3
  778.6 161.1 %reduce-scatter.23.cloned.1.call-done = f32[8,2,512]{2,0,1:T(8,128)} async-done(((f32[512,2,512]{2,0,1:T(8,128)}), f32[8,2,512]{2,0,1:T(8,128)}) %reduce-scatter.23.cloned.1.call-update) | async-done | bytes 32784 | tf_op jit(solution)/shard_map/reduce_scatter | solution.py:56
  940.5 34.0 %psum.31 = bf16[8,2,512]{2,0,1:T(8,128)(2,1)S(1)} all-reduce(bf16[8,2,512]{2,0,1:T(8,128)(2,1)S(1)} %convert_element_type.112), channel_id=1, replica_groups=mesh['rows'=64,'cols'=12] {'cols'}, use_global_device_ids=true, to_apply=%region_11.12 | all-reduce | flops 8192 | bytes 32768 | tf_op jit(solution)/shard_map/psum | solution.py:57
  (50 shorter events, 9.8 us)
Async XLA Ops:
  7.2 13.9 %copy-start = (bf16[12,1,32,2048]{3,2,1,0:T(8,128)(2,1)S(1)}, bf16[12,1,32,2048]{3,2,1,0:T(8,128)(2,1)}, u32[]{:S(2)}) copy-start(bf16[12,1,32,2048]{3,2,1,0:T(8,128)(2,1)} %param.7) | copy-start | bytes 4718596
  7.2 72.9 %reduce-scatter.31.cloned.1.call-start = ((), (), s32[]{:S(2)}) async-start(), calls=%async_computation.15 | async-start | bytes 425984 | tf_op jit(solution)/shard_map/reduce_scatter | solution.py:38
  23.3 115.1 %reduce-scatter.29.cloned.1.call-start = ((), (), s32[]{:S(2)}) async-start(), calls=%async_computation.14 | async-start | bytes 425984 | tf_op jit(solution)/shard_map/reduce_scatter | solution.py:38
  27.2 274.0 %reduce-scatter.17.cloned.1.call-start = ((), (), s32[]{:S(2)}) async-start(), calls=%async_computation.8 | async-start | bytes 2129920 | tf_op jit(solution)/shard_map/reduce_scatter | solution.py:56
  28.6 2.8 copy-start.4
  28.6 4.1 copy-start.2
  87.4 269.9 %reduce-scatter.27.cloned.1.call-start = ((), (), s32[]{:S(2)}) async-start(), calls=%async_computation.13 | async-start | bytes 425984 | tf_op jit(solution)/shard_map/reduce_scatter | solution.py:38
  91.3 428.8 %reduce-scatter.19.cloned.1.call-start = ((), (), s32[]{:S(2)}) async-start(), calls=%async_computation.9 | async-start | bytes 2129920 | tf_op jit(solution)/shard_map/reduce_scatter | solution.py:56
  92.5 244.1 %copy-start.3 = (f32[4,8,512]{2,1,0:T(8,128)S(1)}, f32[4,8,512]{2,1,0:T(8,128)}, u32[]{:S(2)}) copy-start(f32[4,8,512]{2,1,0:T(8,128)} %param.10) | copy-start | bytes 196612
  341.5 234.6 %reduce-scatter.25.cloned.1.call-start = ((), (), s32[]{:S(2)}) async-start(), calls=%async_computation.12 | async-start | bytes 425984 | tf_op jit(solution)/shard_map/reduce_scatter | solution.py:38
  345.5 393.8 %reduce-scatter.21.cloned.1.call-start = ((), (), s32[]{:S(2)}) async-start(), calls=%async_computation.10 | async-start | bytes 2129920 | tf_op jit(solution)/shard_map/reduce_scatter | solution.py:56
  560.6 379.2 %reduce-scatter.23.cloned.1.call-start = ((), (), s32[]{:S(2)}) async-start(), calls=%async_computation.11 | async-start | bytes 2129920 | tf_op jit(solution)/shard_map/reduce_scatter | solution.py:56
  774.2 2.1 copy-start.1
Sparse Core Ops, SparseCore 0:
  23.4 56.6 reduce-scatter.30
  83.5 54.8 reduce-scatter.28
  143.6 157.5 reduce-scatter.16
  304.4 52.9 reduce-scatter.26
  362.4 157.6 reduce-scatter.18
  523.4 52.6 reduce-scatter.24
  581.3 157.8 reduce-scatter.20
  778.0 161.6 reduce-scatter.22
where the time goes:
time: 998 us; the launch traced here: 982 us
  waiting for transfers between devices  751 us (75%)
  blocking collectives  138 us (14%)
  matrix products  46.1 us (5%)
  other arithmetic  19.6 us (2%)
  between operations  14.4 us (1%)
  local copies, waits for them, and re-layouts  12.9 us (1%)
    reduce_scatter x4, waiting for transfers between devices, local(): reduced = lax.psum_scatter(joined, 'rows', scatter_dimension=0, tiled=True)  635 us
    psum x4, blocking collectives, local(): reduced = lax.psum(reduced.astype(jnp.bfloat16), 'cols').astype(jnp.float32)  138 us
    reduce_scatter x4, waiting for transfers between devices, local(): lax.psum_scatter(jnp.dot(known_rows, panel_slab[section], preferred_eleme...  116 us
  transfers between devices with their start and end apart: 8, of which 8 were waited for; matrix products, arithmetic and copies ran while one was open for 6% of the time, Pallas kernels for 0%

commit v1 on v0

v1 whole, which is shorter than its diff:
```python
import functools

import jax
import jax.numpy as jnp
from jax import lax
from jax.experimental import pallas as pl
from jax.experimental.pallas import tpu as pltpu
from jax.sharding import PartitionSpec as P

BF = jnp.bfloat16
F32 = jnp.float32
MESH = pl.DeviceIdType.MESH
SUP = 4


def mm(a, b):
    return jnp.dot(a, b, preferred_element_type=F32)


def mm_t(a, b):
    return lax.dot_general(a, b, (((1,), (1,)), ((), ())), preferred_element_type=F32)


def fold(x):
    half = x.shape[1] // 2
    return jnp.concatenate([x[:, :half], x[:, half:]], axis=0)


def unfold(x):
    rows = x.shape[0] // 2
    return jnp.concatenate([x[:rows], x[rows:]], axis=1)


def kernel(nz, ny, nx, g_h, m_h, l_h, d_h, top_h, td_h, ml_h, pat, cols_h, diag_h, sub_h,
           gv, mv, lv, dv, topv, mlv, pv, rss, rsr, s1, r1, s2, zb, ds, da, fs, fr, tz, ts, tr,
           us, ur, ags, agr, nout, dout, sout,
           in_sem, out_sem, rs_ss, rs_rs, a1_ss, a1_rs, a2_ss, a2_rs, da_ss, da_rs, db_ss, db_rs,
           f_ss, f_rs, t_ss, t_rs, u_ss, u_rs, g_ss, g_rs):
    row = lax.axis_index("rows")
    c = lax.axis_index("cols")
    y = row // nx
    xc = row % nx
    pe = topv.shape[0]
    w = topv.shape[1]
    dc = w // (ny * nx)
    mp = 12 // nz
    seg = nx * pe

    def load(i, src, dst):
        return pltpu.make_async_copy(src, dst, in_sem.at[i])

    loads = {
        "g": load(0, g_h, gv), "ml": load(1, ml_h, mlv), "top": load(2, top_h, topv),
        "d": load(3, d_h, dv.at[pl.ds(0, 4)]), "td": load(4, td_h, dv.at[4]),
    }
    for k in range(SUP):
        loads["m%d" % k] = load(5 + k, m_h.at[k], mv.at[k])
        loads["l%d" % k] = load(9 + k, l_h.at[k], lv.at[k])
    for name in ("ml", "g", "m3", "m2", "m1", "m0", "top", "l3", "l2", "l1", "l0", "d", "td"):
        loads[name].start()

    def rcopy(src, dst, ss, rs, trow, tcol):
        return pltpu.make_async_remote_copy(src_ref=src, dst_ref=dst, send_sem=ss, recv_sem=rs,
                                            device_id=(trow, tcol), device_id_type=MESH)

    def xrow(p):
        return y * nx + (xc + p) % nx

    def yrow(p):
        return ((y + p) % ny) * nx + xc

    bar = pltpu.get_barrier_semaphore()

    def sig(trow, tcol):
        pl.semaphore_signal(bar, inc=1, device_id=(trow, tcol), device_id_type=MESH)

    def over(n, f):
        def body(p, carry):
            f(p)
            return carry
        lax.fori_loop(1, n, body, 0)

    over(nx, lambda p: sig(xrow(p), c))
    over(ny, lambda p: sig(yrow(p), c))
    over(nz, lambda p: sig(row, (c + p) % nz))
    tz[...] = jnp.zeros_like(tz)
    pl.semaphore_wait(bar, (nx - 1) + (ny - 1) + (nz - 1))

    hi, lo = nz // 2, (nz - 1) // 2

    def hops(k, d):
        return lo + (k + d) % 2 if hi != lo else hi

    def rs_copy(k, d, s):
        to = (c + 1) % nz if d == 0 else (c + nz - 1) % nz
        return rcopy(rss.at[k, d, s], rsr.at[k, d, s], rs_ss.at[k, d, s], rs_rs.at[k, d, s], row, to)

    def rs_dest(k, d, s):
        h = hops(k, d) - s
        return (c + h) % nz if d == 0 else (c + nz - h) % nz

    def rs_step(k, d, s):
        val = pv[k, rs_dest(k, d, s)]
        if s > 0:
            rs_copy(k, d, s - 1).wait_recv()
            val = val + rsr[k, d, s - 1].astype(F32)
        rss[k, d, s] = val.astype(BF)
        rs_copy(k, d, s).start()

    loads["ml"].wait()
    loads["g"].wait()

    def first(kk, carry):
        k = 3 - kk
        pltpu.make_async_copy(m_h.at[k], mv.at[k], in_sem.at[5 + k]).wait()
        lhs = gv[...] * mlv[pl.ds(k, 1), :].astype(BF)
        pv[k] = mm(lhs, mv[k]).reshape(nz, pe, w)
        rs_step(k, 0, 0)
        rs_step(k, 1, 0)
        return carry

    lax.fori_loop(0, SUP, first, 0)

    for name in ("top", "l3", "l2", "l1", "l0", "d", "td"):
        loads[name].wait()

    ysrc = c % ny
    ds[...] = jnp.concatenate([dv[4], dv[3], dv[2], dv[1]], axis=0).astype(BF)

    def da_copy(p):
        return rcopy(ds, da.at[xc], da_ss.at[p], da_rs, yrow(p), c)

    @pl.when(y == ysrc)
    def _():
        over(ny, lambda p: da_copy(p).start())
        da[xc] = ds[...]

    def a1_copy(g, p):
        return rcopy(s1.at[g, (xc + p) % nx], r1.at[g, xc], a1_ss.at[g, p], a1_rs.at[g, p], xrow(p), c)

    def a1_wait(g, p):
        src = (xc + nx - p) % nx
        rcopy(s1.at[g, src], r1.at[g, src], a1_ss.at[g, p], a1_rs.at[g, p], xrow(p), c).wait_recv()

    def a2_copy(g, p):
        return rcopy(s2.at[g, (y + p) % ny], zb.at[g, :, pl.ds(pl.multiple_of(y * seg, seg), seg)],
                     a2_ss.at[g, p], a2_rs.at[g, p], yrow(p), c)

    def a2_wait(g, p):
        src = (y + ny - p) % ny
        rcopy(s2.at[g, src], zb.at[g, :, pl.ds(pl.multiple_of(src * seg, seg), seg)],
              a2_ss.at[g, p], a2_rs.at[g, p], yrow(p), c).wait_recv()

    def stage1(g, arrays):
        stack = jnp.concatenate(arrays, axis=0)
        t = stack.T.reshape(ny, nx, dc, 4 * pe)
        for q in range(nx):
            s1[g, q] = t[:, q].reshape(ny * dc, 4 * pe).astype(BF)
        over(nx, lambda p: a1_copy(g, p).start())
        r1[g, xc] = s1[g, xc]

    lane_block = lax.broadcasted_iota(jnp.int32, (ny * dc, 4 * pe), 1) // pe

    def stage2(g):
        over(nx, lambda p: a1_wait(g, p))
        for h in range(nx // 4):
            x = [r1[g, 4 * h + q].astype(F32) for q in range(4)]
            outs = []
            for t in range(4):
                acc = None
                for q in range(4):
                    sh = (pe * (q - t)) % (4 * pe)
                    v = pltpu.roll(x[q], sh, 1) if sh else x[q]
                    acc = v if acc is None else jnp.where(lane_block == q, v, acc)
                outs.append(acc.reshape(ny, dc, 4 * pe))
            both = jnp.stack(outs, axis=1).reshape(ny, 4 * dc, 4 * pe)
            s2[g, :, :, 4 * pe * h:4 * pe * (h + 1)] = both.astype(BF)
        over(ny, lambda p: a2_copy(g, p).start())
        zb[g, :, pl.ds(pl.multiple_of(y * seg, seg), seg)] = s2[g, y]

    top = topv[...]
    b43 = mm(top, lv[3])
    b42 = mm(b43.astype(BF), lv[2])
    b41 = mm(b42.astype(BF), lv[1])
    b40 = mm(b41.astype(BF), lv[0])
    stage1(0, [b43, b42, b41, b40])

    def rs_tick(s):
        def body(kk, carry):
            k = 3 - kk
            rs_step(k, 0, s)
            rs_step(k, 1, s)
            return carry
        lax.fori_loop(0, SUP, body, 0)

    def db_copy(p):
        return rcopy(da.at[xc], da.at[xc], db_ss.at[p], db_rs.at[p], xrow(p), c)

    def db_wait(p):
        src = (xc + nx - p) % nx
        rcopy(da.at[src], da.at[src], db_ss.at[p], db_rs.at[p], xrow(p), c).wait_recv()

    state = {}

    def extra_a():
        @pl.when(y != ysrc)
        def _():
            rcopy(ds, da.at[xc], da_ss.at[0], da_rs, row, c).wait_recv()
        over(nx, lambda p: db_copy(p).start())

    def extra_b():
        stage2(0)

    def extra_c():
        eye = (lax.broadcasted_iota(jnp.int32, (dc, w), 1)
               == row * dc + lax.broadcasted_iota(jnp.int32, (dc, w), 0)).astype(F32)
        cur = []
        lefts = {}
        for j in range(1, 5):
            stack = jnp.concatenate([eye] + cur, axis=0).astype(BF)
            res = mm_t(stack, lv[j - 1])
            cur = [res[dc * i:dc * (i + 1)] for i in range(j)]
            lefts[j] = res
        state["lefts"] = lefts

    def extra_d():
        over(nx, db_wait)
        src_row = lax.broadcasted_iota(jnp.int32, (w, nx * 4 * dc), 0)
        lane = lax.broadcasted_iota(jnp.int32, (w, nx * 4 * dc), 1)
        want = (ysrc * nx + lane // (4 * dc)) * dc + lane % dc
        own = lane // dc % 4
        parts = []
        for j in range(4, 0, -1):
            pick = jnp.where((src_row == want) & (own == 4 - j), 1.0, 0.0).astype(BF)
            parts.append(mm(state["lefts"][j].astype(BF), pick))
        full = jnp.concatenate(parts, axis=0).astype(BF)
        dx = mm(full, da[...].reshape(nx * 4 * dc, w))
        state["dx"] = jnp.where(c < ny, dx, 0.0)

    extras = [extra_a, extra_b, extra_c, extra_d]
    for s in range(1, hi):
        if lo > s or hi == lo:
            rs_tick(s)
        else:
            for k in (3, 2, 1, 0):
                for d in range(2):
                    if s < hops(k, d):
                        rs_step(k, d, s)
        if extras:
            extras.pop(0)()
    for f in extras:
        f()

    def product(k):
        out = pv[k, c]
        for d in range(2):
            h = hops(k, d)
            if h > 0:
                rs_copy(k, d, h - 1).wait_recv()
                out = out + rsr[k, d, h - 1].astype(F32)
        return out

    def finish(k, carried):
        own_mask = pat[k, c * (ny * nx) + row].astype(F32)
        new = (-(product(k) + carried) * own_mask).astype(BF)
        nout[k] = new
        return new

    n3 = finish(3, b43)
    b32 = mm(n3, lv[2])
    n2 = finish(2, b32)
    lev = mm(jnp.concatenate([b32.astype(BF), n2], axis=0), lv[1])
    b31, b21 = lev[:pe], lev[pe:]
    n1 = finish(1, b21)
    lev = mm(jnp.concatenate([b31.astype(BF), b21.astype(BF), n1], axis=0), lv[0])
    b30, b20, b10 = lev[:pe], lev[pe:2 * pe], lev[2 * pe:]
    stage1(1, [n3.astype(F32), b32, b31, b30])
    stage1(2, [n2.astype(F32), b21, b20, top.astype(F32)])
    n0 = finish(0, b10)
    stage1(3, [n1.astype(F32), b10, n0.astype(F32), jnp.zeros((pe, w), F32)])
    out_n = pltpu.make_async_copy(nout, cols_h, out_sem.at[0])
    out_n.start()
    stage2(1)
    stage2(2)
    stage2(3)

    def zmul(k, g0, g1):
        rows = 4 * dc * (g1 - g0)
        z = zb[g0:g1].reshape(rows, ny * seg)
        return mm(z * mlv[k:k + 1, :].astype(BF), mv[k])

    for g in range(3):
        over(ny, lambda p: a2_wait(g, p))
    o3 = zmul(3, 0, 3)
    o2 = zmul(2, 1, 3)
    over(ny, lambda p: a2_wait(3, p))
    o1 = zmul(1, 2, 4)
    o0 = zmul(0, 3, 4)

    def sl(o, i, n=1):
        return o[dc * i:dc * (i + n)]

    dx = state["dx"]
    zero = jnp.zeros((dc, w), F32)
    u = mm(sl(dx, 0, 4).astype(BF), lv[3]) + sl(o3, 0, 4)
    u = u + jnp.concatenate([zero, sl(dx, 4, 3)], axis=0)
    v = sl(o3, 4, 4)
    s3 = sl(o3, 11)
    w_u, w_v, w_s = [None] * 4, [None] * 4, [None] * 4
    w_u[3], w_v[3], w_s[3] = sl(u, 0), sl(v, 0), s3
    lev = mm(jnp.concatenate([sl(u, 1, 3), sl(v, 1, 3)], axis=0).astype(BF), lv[2])
    u = sl(lev, 0, 3) + sl(o2, 1, 3) + jnp.concatenate([zero, sl(dx, 7, 2)], axis=0)
    v = sl(lev, 3, 3) + sl(o2, 4, 3)
    w_u[2], w_v[2], w_s[2] = sl(u, 0), sl(v, 0), sl(o2, 0)
    lev = mm(jnp.concatenate([sl(u, 1, 2), sl(v, 1, 2)], axis=0).astype(BF), lv[1])
    u = sl(lev, 0, 2) + sl(o1, 1, 2) + jnp.concatenate([zero, sl(dx, 9, 1)], axis=0)
    v = sl(lev, 2, 2) + sl(o1, 4, 2)
    w_u[1], w_v[1], w_s[1] = sl(u, 0), sl(v, 0), sl(o1, 0)
    lev = mm(jnp.concatenate([sl(u, 1, 1), sl(v, 1, 1)], axis=0).astype(BF), lv[0])
    w_u[0] = sl(lev, 0) + sl(o0, 1)
    w_v[0] = sl(lev, 1) + sl(o0, 2)
    w_s[0] = sl(o0, 0)

    for k in range(SUP):
        fs[k] = fold(-w_v[k]).astype(BF)
        fs[4 + k] = fold(w_u[k]).astype(BF)
        fs[8 + k] = fold(w_s[k]).astype(BF)

    def f_copy(p):
        to = (c + p) % nz
        return rcopy(fs.at[pl.ds(to * mp, mp)], fr.at[c], f_ss.at[p], f_rs.at[p], row, to)

    def f_wait(p):
        src = (c + nz - p) % nz
        rcopy(fs.at[pl.ds(src * mp, mp)], fr.at[src], f_ss.at[p], f_rs.at[p], row, src).wait_recv()

    over(nz, lambda p: f_copy(p).start())
    fr[c] = fs[pl.ds(c * mp, mp)]
    over(nz, f_wait)
    total = jnp.sum(fr[...].astype(F32), axis=0)

    tl = tz.shape[0]
    off = pl.multiple_of((y % 2 * nx + xc) * dc, dc)
    for q in range(mp):
        tz[pl.ds(off, dc), :] = unfold(total[q])
        t = tz[...].T.reshape(ny, nx, dc, tl)
        for i in range(nx):
            ts[i, q] = t[:, i].reshape(ny * dc, tl).astype(BF)

    def t_copy(p):
        return rcopy(ts.at[(xc + p) % nx], tr.at[xc], t_ss.at[p], t_rs.at[p], xrow(p), c)

    def t_wait(p):
        src = (xc + nx - p) % nx
        rcopy(ts.at[src], tr.at[src], t_ss.at[p], t_rs.at[p], xrow(p), c).wait_recv()

    over(nx, lambda p: t_copy(p).start())
    tr[xc] = ts[xc]
    over(nx, t_wait)
    got = jnp.sum(tr[...].astype(F32), axis=0)
    for q in range(mp):
        us[:, q] = got[q].reshape(ny, dc, tl)

    def u_copy(p):
        return rcopy(us.at[(y + p) % ny], ur.at[y], u_ss.at[p], u_rs.at[p], yrow(p), c)

    def u_wait(p):
        src = (y + ny - p) % ny
        rcopy(us.at[src], ur.at[src], u_ss.at[p], u_rs.at[p], yrow(p), c).wait_recv()

    over(ny, lambda p: u_copy(p).start())
    ur[y] = us[y]
    over(ny, u_wait)
    for q in range(mp):
        flipped = jnp.concatenate([ur[2 * i, q] + ur[2 * i + 1, q] for i in range(ny // 2)], axis=1)
        ags[q] = jnp.where(c * mp + q < 4, fold(flipped), total[q]).astype(BF)

    def g_copy(p):
        return rcopy(ags, agr.at[pl.ds(c * mp, mp)], g_ss.at[p], g_rs.at[p], row, (c + p) % nz)

    def g_wait(p):
        src = (c + nz - p) % nz
        rcopy(ags, agr.at[pl.ds(src * mp, mp)], g_ss.at[p], g_rs.at[p], row, src).wait_recv()

    over(nz, lambda p: g_copy(p).start())
    agr[pl.ds(c * mp, mp)] = ags[...]
    over(nz, g_wait)

    for k in range(SUP):
        dout[k] = dv[k] + unfold(agr[k].astype(F32)) + unfold(agr[4 + k].astype(F32))
    for k in range(SUP):
        prev = dout[k + 1] if k < 3 else dv[4]
        big = prev.astype(BF)
        small = (prev - big.astype(F32)).astype(BF)
        both = mm(jnp.concatenate([big, small], axis=0), lv[k])
        sout[k] = -(unfold(agr[8 + k].astype(F32)) + both[:dc] + both[dc:])
    out_d = pltpu.make_async_copy(dout, diag_h, out_sem.at[1])
    out_s = pltpu.make_async_copy(sout, sub_h, out_sem.at[2])
    out_d.start()
    out_s.start()

    for s in range(hi):
        for k in range(SUP):
            for d in range(2):
                if s < hops(k, d):
                    rs_copy(k, d, s).wait_send()

    @pl.when(y == ysrc)
    def _():
        over(ny, lambda p: da_copy(p).wait_send())

    def drain_x(p):
        db_copy(p).wait_send()
        t_copy(p).wait_send()
        for g in range(4):
            a1_copy(g, p).wait_send()

    def drain_y(p):
        u_copy(p).wait_send()
        for g in range(4):
            a2_copy(g, p).wait_send()

    def drain_z(p):
        f_copy(p).wait_send()
        g_copy(p).wait_send()

    over(nx, drain_x)
    over(ny, drain_y)
    over(nz, drain_z)
    out_n.wait()
    out_d.wait()
    out_s.wait()


def local(known_inverse, lower_panel, chain_panel, diag_inverse, top_cols, top_diag, pattern):
    nr = lax.axis_size("rows")
    nz = lax.axis_size("cols")
    col = lax.axis_index("cols")
    nx = 8 if nr >= 64 else 4
    ny = nr // nx
    pe = known_inverse.shape[2]
    w = lower_panel.shape[-1]
    dc = w // nr
    mp = 12 // nz
    ub = nr * pe
    seg = nx * pe
    hi = nz // 2
    g = known_inverse.reshape(nz * pe, ub)
    m = lower_panel.reshape(SUP, ub, w)
    top = top_cols.reshape(pe, w)
    lanes = jnp.repeat(lax.dynamic_slice_in_dim(pattern, col * nr, nr, 1).astype(F32), pe, axis=1)
    tl = 2 * nx * dc
    dma = pltpu.SemaphoreType.DMA
    vm = pltpu.VMEM
    any_spec = pl.BlockSpec(memory_space=pl.ANY)
    scratch = [
        vm((nz * pe, ub), BF), vm((SUP, ub, w), BF), vm((SUP, w, w), BF), vm((SUP + 1, dc, w), F32),
        vm((pe, w), BF), vm((SUP, ub), F32), vm((SUP, nz, pe, w), F32),
        vm((SUP, 2, hi, pe, w), BF), vm((SUP, 2, hi, pe, w), BF),
        vm((4, nx, ny * dc, 4 * pe), BF), vm((4, nx, ny * dc, 4 * pe), BF),
        vm((4, ny, 4 * dc, seg), BF), vm((4, 4 * dc, ub), BF),
        vm((4 * dc, w), BF), vm((nx, 4 * dc, w), BF),
        vm((12, 2 * dc, w // 2), BF), vm((nz, mp, 2 * dc, w // 2), BF),
        vm((tl, w), F32), vm((nx, mp, ny * dc, tl), BF), vm((nx, mp, ny * dc, tl), BF),
        vm((ny, mp, dc, tl), F32), vm((ny, mp, dc, tl), F32),
        vm((mp, 2 * dc, w // 2), BF), vm((12, 2 * dc, w // 2), BF),
        vm((SUP, pe, w), BF), vm((SUP, dc, w), F32), vm((SUP, dc, w), F32),
        dma((13,)), dma((3,)), dma((SUP, 2, hi)), dma((SUP, 2, hi)),
        dma((4, nx)), dma((4, nx)), dma((4, ny)), dma((4, ny)),
        dma((ny,)), dma(()), dma((nx,)), dma((nx,)),
        dma((nz,)), dma((nz,)), dma((nx,)), dma((nx,)), dma((ny,)), dma((ny,)), dma((nz,)), dma((nz,)),
    ]
    cols, diag, sub = pl.pallas_call(
        functools.partial(kernel, nz, ny, nx),
        out_shape=(
            jax.ShapeDtypeStruct((SUP, pe, w), BF),
            jax.ShapeDtypeStruct((SUP, dc, w), F32),
            jax.ShapeDtypeStruct((SUP, dc, w), F32),
        ),
        in_specs=[any_spec] * 7 + [pl.BlockSpec(memory_space=pltpu.SMEM)],
        out_specs=(any_spec,) * 3,
        scratch_shapes=scratch,
        compiler_params=pltpu.CompilerParams(
            collective_id=0, has_side_effects=True, vmem_limit_bytes=48 * 1024 * 1024
        ),
        name="chain",
    )(g, m, chain_panel, diag_inverse, top, top_diag, lanes, pattern)
    return cols.reshape(SUP, 1, 1, pe, w), diag, sub


def solution(mesh):
    in_specs = (
        P(None, "rows", None, "cols"),
        P(None, "cols", None, None, None),
        P(),
        P(None, "rows", None),
        P("cols", "rows", None, None),
        P("rows", None),
        P(),
    )
    out_specs = (P(None, "cols", "rows", None, None), P(None, "rows", None), P(None, "rows", None))
    return jax.shard_map(local, mesh=mesh, in_specs=in_specs, out_specs=out_specs, check_vma=False)
```

time: 998 us -> 98.6 us (0.10); the launches traced: 982 us -> 98.2 us
  waiting for transfers between devices: 751 us -> 0 us
  blocking collectives: 138 us -> 0 us
  Pallas kernels: 0 us -> 88.6 us
  matrix products: 46.1 us -> 0 us
  other arithmetic: 19.6 us -> 0.76 us
  between operations: 14.4 us -> 0.68 us
    reduce_scatter x8 -> x0, waiting for transfers between devices: 751 us -> none  [the longest x4 635 us: local(): reduced = lax.psum_scatter(joined, 'rows', scatter_dimension=0, tiled=True)]
    psum x4 -> x0, blocking collectives: 138 us -> none  [local(): reduced = lax.psum(reduced.astype(jnp.bfloat16), 'cols').astype(jnp.float32)]
    pallas_call x0 -> x1, Pallas kernels: none -> 88.6 us  [local(): pl.pallas_call(functools.partial(kernel, nz, ny, nx), out_shape=(jax.Shap...]
    dot_general x28 -> x0, matrix products: 46.1 us -> none  [the longest x4 9.94 us: local(): jnp.dot(known_rows, panel_slab[section], preferred_element_type=jnp.float32)]
  transfers between devices with their start and end apart: 8 -> 0, of which waited for: 8 -> 0; matrix products, arithmetic and copies ran while one was open for 6% -> 0% of each run, Pallas kernels for 0% -> 0%
where the time goes in v1:
time: 98.6 us; the launch traced here: 98.2 us
  Pallas kernels  88.6 us (90%)
  local copies, waits for them, and re-layouts  8.14 us (8%)
    pallas_call x1, Pallas kernels, local(): pl.pallas_call(functools.partial(kernel, nz, ny, nx), out_shape=(jax.Shap...  88.6 us
    unnamed x15, local copies, waits for them, and re-layouts  7.93 us

profile of v1, /device:TPU:1, one launch (start us, length us, event | category | flops | bytes accessed | tf_op | source)
XLA Modules:
  0.0 98.2 jit_solution(13923697782766829837)
XLA Ops:
  0.6 0.8 dynamic-slice_convert_fusion
  1.4 0.1 broadcast_in_dim.3
  1.5 0.1 reshape.24.ml_h
  1.6 0.0 copy-start
  1.6 1.6 %copy-done = bf16[4,512,512]{2,1,0:T(8,128)(2,1)S(1)} copy-done((bf16[4,512,512]{2,1,0:T(8,128)(2,1)S(1)}, bf16[4,512,512]{2,1,0:T(8,128)(2,1)}, u32[]{:S(2)}) %copy-start) | copy-done | bytes 2097176
  3.2 0.0 copy-start.1
  3.2 1.4 %copy-done.1 = bf16[12,1,32,2048]{3,2,1,0:T(8,128)(2,1)S(1)} copy-done((bf16[12,1,32,2048]{3,2,1,0:T(8,128)(2,1)S(1)}, bf16[12,1,32,2048]{3,2,1,0:T(8,128)(2,1)}, u32[]{:S(2)}) %copy-start.1) | copy-done | bytes 1572888
  4.6 0.0 copy-start.2
  4.6 0.8 copy-done.2
  5.5 0.0 copy-start.3
  5.5 0.8 copy-done.3
  6.2 0.0 copy-start.4
  6.2 0.7 copy-done.4
  6.9 0.0 copy-start.5
  6.9 0.7 copy-done.5
  7.6 88.6 %chain.1 = (bf16[4,32,512]{2,1,0:T(8,128)(2,1)S(1)}, f32[4,8,512]{2,1,0:T(8,128)S(1)}, f32[4,8,512]{2,1,0:T(8,128)S(1)}) custom-call(bf16[384,2048]{1,0:T(8,128)(2,1)S(1)} %bitcast.6, bf16[4,2048,512]{2,1,0:T(8,128)(2,1)} %bitcast.9, bf16[4,512,512]{2,1,0:T(8,128)(2,1)S(1)} %copy-done, f32[4,8,512]{2,1,0:T(8,128)S(1)} %copy-done.2, ...), custom_call_target="tpu_custom_call" | custom-call | tf_op jit(solution)/shard_map/chain/pallas_call | solution.py:473
  96.3 0.7 copy.15
  96.9 0.6 copy.16
  97.6 0.6 copy.17
Async XLA Ops:
  1.6 1.6 %copy-start = (bf16[4,512,512]{2,1,0:T(8,128)(2,1)S(1)}, bf16[4,512,512]{2,1,0:T(8,128)(2,1)}, u32[]{:S(2)}) copy-start(bf16[4,512,512]{2,1,0:T(8,128)(2,1)} %l_h.1) | copy-start | bytes 6291460
  3.2 1.4 %copy-start.1 = (bf16[12,1,32,2048]{3,2,1,0:T(8,128)(2,1)S(1)}, bf16[12,1,32,2048]{3,2,1,0:T(8,128)(2,1)}, u32[]{:S(2)}) copy-start(bf16[12,1,32,2048]{3,2,1,0:T(8,128)(2,1)} %param.7) | copy-start | bytes 4718596
  4.6 0.8 copy-start.2
  5.5 0.8 copy-start.3
  6.2 0.7 copy-start.4
  6.9 0.7 copy-start.5

commit v2 on v1

v2 whole, which is shorter than its diff:
```python
import functools

import jax
import jax.numpy as jnp
from jax import lax
from jax.experimental import pallas as pl
from jax.experimental.pallas import tpu as pltpu
from jax.sharding import PartitionSpec as P

BF = jnp.bfloat16
F32 = jnp.float32
MESH = pl.DeviceIdType.MESH
SUP = 4
OFF = {3: 0, 2: 1, 1: 2, 0: 3}


def mm(a, b):
    return jnp.dot(a, b, preferred_element_type=F32)


def mm_t(a, b):
    return lax.dot_general(a, b, (((1,), (1,)), ((), ())), preferred_element_type=F32)


def fold(x):
    half = x.shape[1] // 2
    return jnp.concatenate([x[:, :half], x[:, half:]], axis=0)


def unfold(x):
    rows = x.shape[0] // 2
    return jnp.concatenate([x[:rows], x[rows:]], axis=1)


def plane_w(k, nz):
    return (3 * k) % nz


def plane_s(k, nz):
    return (3 * k + 1) % nz


def kernel(nz, ny, nx, g_h, m_h, l_h, d_h, top_h, td_h, pat, cols_h, diag_h, sub_h,
           gv, mv, lv, dv, topv, mlv, pv, rss, rsr, s1, r1, s2, zb, ds, da, fs, fr, fw, fv, tz, ts, tr,
           us, ur, gs, gw, ags, agw, nout, dout, sout,
           in_sem, out_sem, rs_ss, rs_rs, a1_ss, a1_rs, a2_ss, a2_rs, da_ss, da_rs, db_ss, db_rs,
           f_ss, f_rs, w_ss, w_rs, t_ss, t_rs, u_ss, u_rs, g_ss, g_rs, h_ss, h_rs):
    row = lax.axis_index("rows")
    c = lax.axis_index("cols")
    y = row // nx
    xc = row % nx
    pe = topv.shape[0]
    w = topv.shape[1]
    dc = w // (ny * nx)
    seg = nx * pe

    def load(i, src, dst):
        return pltpu.make_async_copy(src, dst, in_sem.at[i])

    loads = {
        "g": load(0, g_h, gv), "top": load(2, top_h, topv),
        "d": load(3, d_h, dv.at[pl.ds(0, 4)]), "td": load(4, td_h, dv.at[4]),
    }
    for k in range(SUP):
        loads["m%d" % k] = load(5 + k, m_h.at[k], mv.at[k])
        loads["l%d" % k] = load(9 + k, l_h.at[k], lv.at[k])
    loads["g"].start()
    loads["m3"].start()

    def rcopy(src, dst, ss, rs, trow, tcol):
        return pltpu.make_async_remote_copy(src_ref=src, dst_ref=dst, send_sem=ss, recv_sem=rs,
                                            device_id=(trow, tcol), device_id_type=MESH)

    def xrow(p):
        return y * nx + (xc + p) % nx

    def yrow(p):
        return ((y + p) % ny) * nx + xc

    bar = pltpu.get_barrier_semaphore()

    def sig(trow, tcol):
        pl.semaphore_signal(bar, inc=1, device_id=(trow, tcol), device_id_type=MESH)

    def over(n, f):
        def body(p, carry):
            f(p)
            return carry
        lax.fori_loop(1, n, body, 0)

    over(nx, lambda p: sig(xrow(p), c))
    over(ny, lambda p: sig(yrow(p), c))
    over(nz, lambda p: sig(row, (c + p) % nz))
    lane = lax.broadcasted_iota(jnp.int32, (1, 128), 1) // pe

    def mask_lanes(v, carry):
        for k in range(SUP):
            val = jnp.zeros((1, 128), F32)
            for q in range(128 // pe):
                one = pat[k, c * (ny * nx) + v * (128 // pe) + q].astype(F32)
                val = jnp.where(lane == q, one, val)
            mlv[pl.ds(k, 1), pl.ds(pl.multiple_of(v * 128, 128), 128)] = val
        return carry

    lax.fori_loop(0, ny * nx * pe // 128, mask_lanes, 0)
    tz[...] = jnp.zeros_like(tz)
    loads["g"].wait()
    pl.semaphore_wait(bar, (nx - 1) + (ny - 1) + (nz - 1))

    hi, lo = nz // 2, (nz - 1) // 2

    def hops(k, d):
        return lo + (k + d) % 2 if hi != lo else hi

    def rs_copy(k, d, s):
        to = (c + 1) % nz if d == 0 else (c + nz - 1) % nz
        return rcopy(rss.at[k, d, s], rsr.at[k, d, s], rs_ss.at[k, d, s], rs_rs.at[k, d, s], row, to)

    def rs_dest(k, d, s):
        h = hops(k, d) - s
        return (c + h) % nz if d == 0 else (c + nz - h) % nz

    def rs_step(k, d, s):
        val = pv[k, rs_dest(k, d, s)]
        if s > 0:
            rs_copy(k, d, s - 1).wait_recv()
            val = val + rsr[k, d, s - 1].astype(F32)
        rss[k, d, s] = val.astype(BF)
        rs_copy(k, d, s).start()

    def product_part(k):
        loads["m%d" % k].wait()
        for name in after[k]:
            loads[name].start()
        lhs = gv[...] * mlv[k:k + 1, :].astype(BF)
        pv[k] = mm(lhs, mv[k]).reshape(nz, pe, w)

    after = {3: ("m2", "top", "l3", "l2"), 2: ("m1", "l1", "l0"), 1: ("m0", "d", "td"), 0: ()}

    ysrc = c % ny
    def da_copy(p):
        return rcopy(ds, da.at[xc], da_ss.at[p], da_rs, yrow(p), c)

    def da_send():
        loads["d"].wait()
        loads["td"].wait()
        ds[...] = jnp.concatenate([dv[4], dv[3], dv[2], dv[1]], axis=0).astype(BF)

        @pl.when(y == ysrc)
        def _():
            over(ny, lambda p: da_copy(p).start())
            da[xc] = ds[...]

    def a1_copy(g, p):
        return rcopy(s1.at[g, (xc + p) % nx], r1.at[g, xc], a1_ss.at[g, p], a1_rs.at[g, p], xrow(p), c)

    def a1_wait(g, p):
        src = (xc + nx - p) % nx
        rcopy(s1.at[g, src], r1.at[g, src], a1_ss.at[g, p], a1_rs.at[g, p], xrow(p), c).wait_recv()

    def a2_copy(g, p):
        return rcopy(s2.at[g, (y + p) % ny], zb.at[g, :, pl.ds(pl.multiple_of(y * seg, seg), seg)],
                     a2_ss.at[g, p], a2_rs.at[g, p], yrow(p), c)

    def a2_wait(g, p):
        src = (y + ny - p) % ny
        rcopy(s2.at[g, src], zb.at[g, :, pl.ds(pl.multiple_of(src * seg, seg), seg)],
              a2_ss.at[g, p], a2_rs.at[g, p], yrow(p), c).wait_recv()

    def stage1(g, arrays):
        stack = jnp.concatenate(arrays, axis=0)
        t = stack.T.reshape(ny, nx, dc, 4 * pe)
        for q in range(nx):
            s1[g, q] = t[:, q].reshape(ny * dc, 4 * pe).astype(BF)
        over(nx, lambda p: a1_copy(g, p).start())
        r1[g, xc] = s1[g, xc]

    lane_block = lax.broadcasted_iota(jnp.int32, (ny * dc, 4 * pe), 1) // pe

    def stage2(g):
        over(nx, lambda p: a1_wait(g, p))
        for h in range(nx // 4):
            x = [r1[g, 4 * h + q].astype(F32) for q in range(4)]
            outs = []
            for t in range(4):
                acc = None
                for q in range(4):
                    sh = (pe * (q - t)) % (4 * pe)
                    v = pltpu.roll(x[q], sh, 1) if sh else x[q]
                    acc = v if acc is None else jnp.where(lane_block == q, v, acc)
                outs.append(acc.reshape(ny, dc, 4 * pe))
            both = jnp.stack(outs, axis=1).reshape(ny, 4 * dc, 4 * pe)
            s2[g, :, :, 4 * pe * h:4 * pe * (h + 1)] = both.astype(BF)
        over(ny, lambda p: a2_copy(g, p).start())
        zb[g, :, pl.ds(pl.multiple_of(y * seg, seg), seg)] = s2[g, y]

    state = {}

    def group0():
        for name in ("top", "l3", "l2", "l1", "l0"):
            loads[name].wait()
        b43 = mm(topv[...], lv[3])
        b42 = mm(b43.astype(BF), lv[2])
        b41 = mm(b42.astype(BF), lv[1])
        b40 = mm(b41.astype(BF), lv[0])
        state["b43"] = b43
        stage1(0, [b43, b42, b41, b40])

    def db_copy(p):
        return rcopy(da.at[xc], da.at[xc], db_ss.at[p], db_rs.at[p], xrow(p), c)

    def db_wait(p):
        src = (xc + nx - p) % nx
        rcopy(da.at[src], da.at[src], db_ss.at[p], db_rs.at[p], xrow(p), c).wait_recv()

    def extra_a():
        @pl.when(y != ysrc)
        def _():
            rcopy(ds, da.at[xc], da_ss.at[0], da_rs, row, c).wait_recv()
        over(nx, lambda p: db_copy(p).start())

    def extra_c():
        eye = (lax.broadcasted_iota(jnp.int32, (dc, w), 1)
               == row * dc + lax.broadcasted_iota(jnp.int32, (dc, w), 0)).astype(F32)
        cur = []
        lefts = {}
        for j in range(1, 5):
            stack = jnp.concatenate([eye] + cur, axis=0).astype(BF)
            res = mm_t(stack, lv[j - 1])
            cur = [res[dc * i:dc * (i + 1)] for i in range(j)]
            lefts[j] = res
        state["lefts"] = lefts

    def extra_d():
        over(nx, db_wait)
        src_row = lax.broadcasted_iota(jnp.int32, (w, nx * 4 * dc), 0)
        lane = lax.broadcasted_iota(jnp.int32, (w, nx * 4 * dc), 1)
        want = (ysrc * nx + lane // (4 * dc)) * dc + lane % dc
        own = lane // dc % 4
        parts = []
        for j in range(4, 0, -1):
            pick = jnp.where((src_row == want) & (own == 4 - j), 1.0, 0.0).astype(BF)
            parts.append(mm(state["lefts"][j].astype(BF), pick))
        full = jnp.concatenate(parts, axis=0).astype(BF)
        dx = mm(full, da[...].reshape(nx * 4 * dc, w))
        state["dx"] = jnp.where(c < ny, dx, 0.0)

    def product(k):
        out = pv[k, c]
        for d in range(2):
            h = hops(k, d)
            if h > 0:
                rs_copy(k, d, h - 1).wait_recv()
                out = out + rsr[k, d, h - 1].astype(F32)
        return out

    def finish(k, carried):
        own_mask = pat[k, c * (ny * nx) + row].astype(F32)
        new = (-(product(k) + carried) * own_mask).astype(BF)
        nout[k] = new
        return new

    def tail3():
        n3 = finish(3, state["b43"])
        b32 = mm(n3, lv[2])
        b31 = mm(b32.astype(BF), lv[1])
        b30 = mm(b31.astype(BF), lv[0])
        state["b32"] = b32
        stage1(1, [n3.astype(F32), b32, b31, b30])

    def tail2():
        n2 = finish(2, state["b32"])
        b21 = mm(n2, lv[1])
        b20 = mm(b21.astype(BF), lv[0])
        state["b21"] = b21
        stage1(2, [n2.astype(F32), b21, b20, topv[...].astype(F32)])

    def tail1():
        n1 = finish(1, state["b21"])
        state["n1"] = n1
        state["b10"] = mm(n1, lv[0])

    def tail0():
        n0 = finish(0, state["b10"])
        stage1(3, [state["n1"].astype(F32), state["b10"], n0.astype(F32), jnp.zeros((pe, w), F32)])

    hooks = {}

    def hook(t, f):
        hooks.setdefault(t, []).append(f)

    end = {k: OFF[k] + hi for k in range(SUP)}
    hook(2, group0)
    hook(3, da_send)
    hook(4, lambda: stage2(0))
    hook(4, extra_a)
    hook(4, extra_c)
    hook(5, extra_d)
    hook(end[3], tail3)
    hook(end[2], tail2)
    hook(max(end[2], end[3] + 1), lambda: stage2(1))
    hook(end[1], tail1)
    hook(end[0], tail0)
    for t in range(max(max(end.values()), max(hooks)) + 1):
        for k in range(SUP):
            if t == OFF[k]:
                product_part(k)
                rs_step(k, 0, 0)
                rs_step(k, 1, 0)
        for k in (3, 2, 1, 0):
            s = t - OFF[k]
            for d in range(2):
                if 0 < s < hops(k, d):
                    rs_step(k, d, s)
        for f in hooks.get(t, ()):
            f()
    out_n = pltpu.make_async_copy(nout, cols_h, out_sem.at[0])
    out_n.start()
    stage2(2)

    def zmul(k, g0, g1):
        rows = 4 * dc * (g1 - g0)
        z = zb[g0:g1].reshape(rows, ny * seg)
        return mm(z * mlv[k:k + 1, :].astype(BF), mv[k])

    for g in range(3):
        over(ny, lambda p: a2_wait(g, p))
    o3 = zmul(3, 0, 3)
    o2 = zmul(2, 1, 3)
    fs[3] = fold(o3[11 * dc:]).astype(BF)
    fs[2] = fold(o2[:dc]).astype(BF)

    def f_copy(k):
        return rcopy(fs.at[k], fr.at[c], f_ss.at[k], f_rs.at[c], row, plane_s(k, nz))

    def f_send(k):
        @pl.when(c != plane_s(k, nz))
        def _():
            f_copy(k).start()

        @pl.when(c == plane_s(k, nz))
        def _():
            fr[c] = fs[k]

    f_send(3)
    f_send(2)
    stage2(3)
    for s in range(hi):
        for k in range(SUP):
            for d in range(2):
                if s < hops(k, d):
                    rs_copy(k, d, s).wait_send()
    over(ny, lambda p: a2_wait(3, p))
    o1 = zmul(1, 2, 4)
    o0 = zmul(0, 3, 4)
    fs[1] = fold(o1[:dc]).astype(BF)
    fs[0] = fold(o0[:dc]).astype(BF)
    f_send(1)
    f_send(0)

    def sl(o, i, n=1):
        return o[dc * i:dc * (i + n)]

    dx = state["dx"]
    zero = jnp.zeros((dc, w), F32)
    u = mm(sl(dx, 0, 4).astype(BF), lv[3]) + sl(o3, 0, 4)
    u = u + jnp.concatenate([zero, sl(dx, 4, 3)], axis=0)
    v = sl(o3, 4, 4)
    w_u, w_v = [None] * 4, [None] * 4
    w_u[3], w_v[3] = sl(u, 0), sl(v, 0)
    lev = mm(jnp.concatenate([sl(u, 1, 3), sl(v, 1, 3)], axis=0).astype(BF), lv[2])
    u = sl(lev, 0, 3) + sl(o2, 1, 3) + jnp.concatenate([zero, sl(dx, 7, 2)], axis=0)
    v = sl(lev, 3, 3) + sl(o2, 4, 3)
    w_u[2], w_v[2] = sl(u, 0), sl(v, 0)
    lev = mm(jnp.concatenate([sl(u, 1, 2), sl(v, 1, 2)], axis=0).astype(BF), lv[1])
    u = sl(lev, 0, 2) + sl(o1, 1, 2) + jnp.concatenate([zero, sl(dx, 9, 1)], axis=0)
    v = sl(lev, 2, 2) + sl(o1, 4, 2)
    w_u[1], w_v[1] = sl(u, 0), sl(v, 0)
    lev = mm(jnp.concatenate([sl(u, 1, 1), sl(v, 1, 1)], axis=0).astype(BF), lv[0])
    w_u[0] = sl(lev, 0) + sl(o0, 1)
    w_v[0] = sl(lev, 1) + sl(o0, 2)

    for k in range(SUP):
        fw[k, 0] = fold(-w_v[k]).astype(BF)
        fw[k, 1] = fold(w_u[k]).astype(BF)

    def w_copy(k):
        return rcopy(fw.at[k], fv.at[c], w_ss.at[k], w_rs.at[c], row, plane_w(k, nz))

    for k in range(SUP):
        @pl.when(c != plane_w(k, nz))
        def _():
            w_copy(k).start()

        @pl.when(c == plane_w(k, nz))
        def _():
            fv[c] = fw[k]

    def from_plane(p):
        return (c + nz - p) % nz

    def g_copy(k, p):
        return rcopy(gs, ags.at[k], g_ss.at[p], g_rs.at[k], row, (c + p) % nz)

    def h_copy(k, p):
        return rcopy(gw, agw.at[k], h_ss.at[p], h_rs.at[k], row, (c + p) % nz)

    for k in range(SUP):
        @pl.when(c == plane_s(k, nz))
        def _():
            def f_wait(p):
                src = from_plane(p)
                rcopy(fs.at[k], fr.at[src], f_ss.at[k], f_rs.at[src], row, src).wait_recv()

            over(nz, f_wait)
            gs[...] = jnp.sum(fr[...].astype(F32), axis=0).astype(BF)
            over(nz, lambda p: g_copy(k, p).start())
            ags[k] = gs[...]

    tl = tz.shape[0]

    def t_copy(p):
        return rcopy(ts.at[(xc + p) % nx], tr.at[xc], t_ss.at[p], t_rs.at[p], xrow(p), c)

    def t_wait(p):
        src = (xc + nx - p) % nx
        rcopy(ts.at[src], tr.at[src], t_ss.at[p], t_rs.at[p], xrow(p), c).wait_recv()

    def u_copy(p):
        return rcopy(us.at[(y + p) % ny], ur.at[y], u_ss.at[p], u_rs.at[p], yrow(p), c)

    def u_wait(p):
        src = (y + ny - p) % ny
        rcopy(us.at[src], ur.at[src], u_ss.at[p], u_rs.at[p], yrow(p), c).wait_recv()

    is_w = c == plane_w(0, nz)
    for k in range(1, SUP):
        is_w = is_w | (c == plane_w(k, nz))

    @pl.when(is_w)
    def _():
        def w_wait(p):
            src = from_plane(p)
            rcopy(fw.at[0], fv.at[src], w_ss.at[0], w_rs.at[src], row, src).wait_recv()

        over(nz, w_wait)
        total = jnp.sum(fv[...].astype(F32), axis=0)
        off = pl.multiple_of((y % 2 * nx + xc) * dc, dc)
        tz[pl.ds(off, dc), :] = unfold(total[0])
        t = tz[...].T.reshape(ny, nx, dc, tl)
        for i in range(nx):
            ts[i] = t[:, i].reshape(ny * dc, tl).astype(BF)
        over(nx, lambda p: t_copy(p).start())
        tr[xc] = ts[xc]
        over(nx, t_wait)
        us[...] = jnp.sum(tr[...].astype(F32), axis=0).reshape(ny, dc, tl)
        over(ny, lambda p: u_copy(p).start())
        ur[y] = us[y]
        over(ny, u_wait)
        flipped = jnp.concatenate([ur[2 * i] + ur[2 * i + 1] for i in range(ny // 2)], axis=1)
        gw[...] = (fold(flipped) + total[1]).astype(BF)

    for k in range(SUP):
        @pl.when(c == plane_w(k, nz))
        def _():
            over(nz, lambda p: h_copy(k, p).start())
            agw[k] = gw[...]

    def drain_x(p):
        db_copy(p).wait_send()
        for g in range(4):
            a1_copy(g, p).wait_send()

    def drain_y(p):
        for g in range(4):
            a2_copy(g, p).wait_send()

    over(nx, drain_x)
    over(ny, drain_y)

    @pl.when(y == ysrc)
    def _():
        over(ny, lambda p: da_copy(p).wait_send())

    for k in range(SUP):
        @pl.when(c != plane_s(k, nz))
        def _():
            f_copy(k).wait_send()
            g_copy(k, 1).wait_recv()

        @pl.when(c != plane_w(k, nz))
        def _():
            w_copy(k).wait_send()

    for k in (3, 2, 1, 0):
        @pl.when(c != plane_w(k, nz))
        def _():
            h_copy(k, 1).wait_recv()

        dout[k] = dv[k] + unfold(agw[k].astype(F32))
    for k in range(SUP):
        prev = dout[k + 1] if k < 3 else dv[4]
        big = prev.astype(BF)
        small = (prev - big.astype(F32)).astype(BF)
        both = mm(jnp.concatenate([big, small], axis=0), lv[k])
        sout[k] = -(unfold(ags[k].astype(F32)) + both[:dc] + both[dc:])
    out_d = pltpu.make_async_copy(dout, diag_h, out_sem.at[1])
    out_s = pltpu.make_async_copy(sout, sub_h, out_sem.at[2])
    out_d.start()
    out_s.start()

    @pl.when(is_w)
    def _():
        over(nx, lambda p: t_copy(p).wait_send())
        over(ny, lambda p: u_copy(p).wait_send())
        over(nz, lambda p: h_copy(0, p).wait_send())

    for k in range(SUP):
        @pl.when(c == plane_s(k, nz))
        def _():
            over(nz, lambda p: g_copy(k, p).wait_send())

    out_n.wait()
    out_d.wait()
    out_s.wait()


def local(known_inverse, lower_panel, chain_panel, diag_inverse, top_cols, top_diag, pattern):
    nr = lax.axis_size("rows")
    nz = lax.axis_size("cols")
    nx = 8 if nr >= 64 else 4
    ny = nr // nx
    pe = known_inverse.shape[2]
    w = lower_panel.shape[-1]
    dc = w // nr
    ub = nr * pe
    seg = nx * pe
    hi = nz // 2
    g = known_inverse.reshape(nz * pe, ub)
    m = lower_panel.reshape(SUP, ub, w)
    top = top_cols.reshape(pe, w)
    tl = 2 * nx * dc
    dma = pltpu.SemaphoreType.DMA
    vm = pltpu.VMEM
    any_spec = pl.BlockSpec(memory_space=pltpu.HBM)
    scratch = [
        vm((nz * pe, ub), BF), vm((SUP, ub, w), BF), vm((SUP, w, w), BF), vm((SUP + 1, dc, w), F32),
        vm((pe, w), BF), vm((SUP, ub), F32), vm((SUP, nz, pe, w), F32),
        vm((SUP, 2, hi, pe, w), BF), vm((SUP, 2, hi, pe, w), BF),
        vm((4, nx, ny * dc, 4 * pe), BF), vm((4, nx, ny * dc, 4 * pe), BF),
        vm((4, ny, 4 * dc, seg), BF), vm((4, 4 * dc, ub), BF),
        vm((4 * dc, w), BF), vm((nx, 4 * dc, w), BF),
        vm((SUP, 2 * dc, w // 2), BF), vm((nz, 2 * dc, w // 2), BF),
        vm((SUP, 2, 2 * dc, w // 2), BF), vm((nz, 2, 2 * dc, w // 2), BF),
        vm((tl, w), F32), vm((nx, ny * dc, tl), BF), vm((nx, ny * dc, tl), BF),
        vm((ny, dc, tl), F32), vm((ny, dc, tl), F32),
        vm((2 * dc, w // 2), BF), vm((2 * dc, w // 2), BF),
        vm((SUP, 2 * dc, w // 2), BF), vm((SUP, 2 * dc, w // 2), BF),
        vm((SUP, pe, w), BF), vm((SUP, dc, w), F32), vm((SUP, dc, w), F32),
        dma((13,)), dma((3,)), dma((SUP, 2, hi)), dma((SUP, 2, hi)),
        dma((4, nx)), dma((4, nx)), dma((4, ny)), dma((4, ny)),
        dma((ny,)), dma(()), dma((nx,)), dma((nx,)),
        dma((SUP,)), dma((nz,)), dma((SUP,)), dma((nz,)), dma((nx,)), dma((nx,)), dma((ny,)), dma((ny,)),
        dma((nz,)), dma((SUP,)), dma((nz,)), dma((SUP,)),
    ]
    cols, diag, sub = pl.pallas_call(
        functools.partial(kernel, nz, ny, nx),
        out_shape=(
            jax.ShapeDtypeStruct((SUP, pe, w), BF),
            jax.ShapeDtypeStruct((SUP, dc, w), F32),
            jax.ShapeDtypeStruct((SUP, dc, w), F32),
        ),
        in_specs=[any_spec] * 6 + [pl.BlockSpec(memory_space=pltpu.SMEM)],
        out_specs=(any_spec,) * 3,
        scratch_shapes=scratch,
        compiler_params=pltpu.CompilerParams(
            collective_id=0, has_side_effects=True, vmem_limit_bytes=64 * 1024 * 1024
        ),
        name="chain",
    )(g, m, chain_panel, diag_inverse, top, top_diag, pattern)
    return cols.reshape(SUP, 1, 1, pe, w), diag, sub


def solution(mesh):
    in_specs = (
        P(None, "rows", None, "cols"),
        P(None, "cols", None, None, None),
        P(),
        P(None, "rows", None),
        P("cols", "rows", None, None),
        P("rows", None),
        P(),
    )
    out_specs = (P(None, "cols", "rows", None, None), P(None, "rows", None), P(None, "rows", None))
    return jax.shard_map(local, mesh=mesh, in_specs=in_specs, out_specs=out_specs, check_vma=False)
```

time: 98.6 us -> 98.5 us (level)
  Pallas kernels: 88.6 us -> 93.1 us
  local copies, waits for them, and re-layouts: 8.14 us -> 4.51 us
    pallas_call x1, Pallas kernels: 88.6 us -> 93.1 us  [local(): pl.pallas_call(functools.partial(kernel, nz, ny, nx), out_shape=(jax.Shap...]
    unnamed x15 -> x3, local copies, waits for them, and re-layouts: 7.93 us -> 4.51 us
where the time goes in v2:
time: 98.5 us; the launch traced here: 98.2 us
  Pallas kernels  93.1 us (95%)
  local copies, waits for them, and re-layouts  4.51 us (5%)
    pallas_call x1, Pallas kernels, local(): pl.pallas_call(functools.partial(kernel, nz, ny, nx), out_shape=(jax.Shap...  93.1 us
    unnamed x3, local copies, waits for them, and re-layouts  4.51 us

profile of v2, /device:TPU:1, one launch (start us, length us, event | category | flops | bytes accessed | tf_op | source)
XLA Modules:
  0.0 98.2 jit_solution(17580235878732257934)
XLA Ops:
  0.6 93.1 %chain.1 = (bf16[4,32,512]{2,1,0:T(8,128)(2,1)}, f32[4,8,512]{2,1,0:T(8,128)}, f32[4,8,512]{2,1,0:T(8,128)}) custom-call(bf16[384,2048]{1,0:T(8,128)(2,1)} %bitcast.7, bf16[4,2048,512]{2,1,0:T(8,128)(2,1)} %bitcast.6, bf16[4,512,512]{2,1,0:T(8,128)(2,1)} %l_h.1, f32[4,8,512]{2,1,0:T(8,128)} %d_h.1, bf16[32,512]{1,0:T(8,128)(2,1)} %bitcast.9, f32[8,512]{1,0:T(8,128)} %td_h.1, ...), custom_call_target="tpu_custom_call" | custom-call | tf_op jit(solution)/shard_map/chain/pallas_call | solution.py:566
  93.7 1.6 %copy.14 = bf16[4,1,1,32,512]{4,3,2,1,0:T(8,128)(2,1)} copy(bf16[4,1,1,32,512]{4,3,2,1,0:T(8,128)(2,1)} %bitcast.8) | data formatting | bytes 262144
  95.3 1.5 %copy.15 = f32[4,8,512]{2,1,0:T(8,128)} copy(f32[4,8,512]{2,1,0:T(8,128)} %get-tuple-element.16) | data formatting | bytes 131072
  96.8 1.5 %copy.16 = f32[4,8,512]{2,1,0:T(8,128)} copy(f32[4,8,512]{2,1,0:T(8,128)} %get-tuple-element.17) | data formatting | bytes 131072

commit v3 on v2

v3 whole, which is shorter than its diff:
```python
import functools

import jax
import jax.numpy as jnp
from jax import lax
from jax.experimental import pallas as pl
from jax.experimental.pallas import tpu as pltpu
from jax.sharding import PartitionSpec as P

BF = jnp.bfloat16
F32 = jnp.float32
MESH = pl.DeviceIdType.MESH
SUP = 4
OFF = {3: 0, 2: 0, 1: 0, 0: 0}


def mm(a, b):
    return jnp.dot(a, b, preferred_element_type=F32)


def mm_t(a, b):
    return lax.dot_general(a, b, (((1,), (1,)), ((), ())), preferred_element_type=F32)


def fold(x):
    half = x.shape[1] // 2
    return jnp.concatenate([x[:, :half], x[:, half:]], axis=0)


def unfold(x):
    rows = x.shape[0] // 2
    return jnp.concatenate([x[:rows], x[rows:]], axis=1)


def plane_w(k, nz):
    return (3 * k) % nz


def plane_s(k, nz):
    return (3 * k + 1) % nz


def tri(j, k):
    return j * (j + 1) // 2 + k


def kernel(nz, ny, nx, g_h, m_h, l_h, d_h, top_h, td_h, pat, cols_h, both_h,
           gv, mv, lv, dv, topv, mlv, pv, rss, rsr, xg, dg, ma, mat, accp, accs, cs, cr, ys, yr,
           fs, fr, fw, fv, gs, gw, ags, agw, nout, dout, sout,
           in_sem, out_sem, rs_ss, rs_rs, x_ss, x_rs, c_ss, c_rs, y_ss, y_rs,
           f_ss, f_rs, w_ss, w_rs, g_ss, g_rs, h_ss, h_rs):
    row = lax.axis_index("rows")
    c = lax.axis_index("cols")
    y = row // nx
    nc = nx // 2
    x = row % nx // 2
    co = row % 2
    pe = topv.shape[0]
    w = topv.shape[1]
    dc = w // (ny * nx)
    ku = nc * pe
    half = ny * dc

    def load(i, src, dst):
        return pltpu.make_async_copy(src, dst, in_sem.at[i])

    loads = {
        "g": load(0, g_h, gv), "top": load(2, top_h, topv),
        "d": load(3, d_h, dv.at[pl.ds(0, 4)]), "td": load(4, td_h, dv.at[4]),
    }
    for k in range(SUP):
        loads["m%d" % k] = load(5 + k, m_h.at[k], mv.at[k])
        loads["l%d" % k] = load(9 + k, l_h.at[k], lv.at[k])
    loads["g"].start()
    loads["m3"].start()

    def rcopy(src, dst, ss, rs, trow, tcol):
        return pltpu.make_async_remote_copy(src_ref=src, dst_ref=dst, send_sem=ss, recv_sem=rs,
                                            device_id=(trow, tcol), device_id_type=MESH)

    def xrow(p):
        return y * nx + (x + p) % nc * 2 + co

    def yrow(p):
        return (y + p) % ny * nx + x * 2 + co

    twin = y * nx + x * 2 + 1 - co

    bar = pltpu.get_barrier_semaphore()

    def sig(trow, tcol):
        pl.semaphore_signal(bar, inc=1, device_id=(trow, tcol), device_id_type=MESH)

    def over(n, f):
        def body(p, carry):
            f(p)
            return carry
        lax.fori_loop(1, n, body, 0)

    over(nc, lambda p: sig(xrow(p), c))
    sig(twin, c)
    over(ny, lambda p: sig(yrow(p), c))
    over(nz, lambda p: sig(row, (c + p) % nz))
    lane = lax.broadcasted_iota(jnp.int32, (1, 128), 1) // pe

    def mask_lanes(v, carry):
        for k in range(SUP):
            val = jnp.zeros((1, 128), F32)
            for q in range(128 // pe):
                one = pat[k, c * (ny * nx) + v * (128 // pe) + q].astype(F32)
                val = jnp.where(lane == q, one, val)
            mlv[pl.ds(k, 1), pl.ds(pl.multiple_of(v * 128, 128), 128)] = val
        return carry

    lax.fori_loop(0, ny * nx * pe // 128, mask_lanes, 0)
    loads["g"].wait()
    pl.semaphore_wait(bar, nc + (ny - 1) + (nz - 1))

    hi, lo = nz // 2, (nz - 1) // 2

    def hops(k, d):
        return lo + (k + d) % 2 if hi != lo else hi

    def rs_copy(k, d, s):
        to = (c + 1) % nz if d == 0 else (c + nz - 1) % nz
        return rcopy(rss.at[k, d, s], rsr.at[k, d, s], rs_ss.at[k, d, s], rs_rs.at[k, d, s], row, to)

    def rs_dest(k, d, s):
        h = hops(k, d) - s
        return (c + h) % nz if d == 0 else (c + nz - h) % nz

    def rs_step(k, d, s):
        val = pv[k, rs_dest(k, d, s)]
        if s > 0:
            rs_copy(k, d, s - 1).wait_recv()
            val = val + rsr[k, d, s - 1].astype(F32)
        rss[k, d, s] = val.astype(BF)
        rs_copy(k, d, s).start()

    def product_part(k):
        loads["m%d" % k].wait()
        for name in after[k]:
            loads[name].start()
        lhs = gv[...] * mlv[k:k + 1, :].astype(BF)
        pv[k] = mm(lhs, mv[k]).reshape(nz, pe, w)

    after = {3: ("m2", "top", "l3", "l2"), 2: ("m1", "l1", "l0"), 1: ("m0", "d", "td"), 0: ()}

    def x_copy(j, p):
        return rcopy(xg.at[j, x], xg.at[j, x], x_ss.at[j, p], x_rs.at[j, p], xrow(p), c)

    def x_wait(j, p):
        src = (x + nc - p) % nc
        rcopy(xg.at[j, src], xg.at[j, src], x_ss.at[j, p], x_rs.at[j, p], xrow(p), c).wait_recv()

    def d_copy(p):
        return rcopy(dg.at[x], dg.at[x], x_ss.at[5, p], x_rs.at[5, p], xrow(p), c)

    def d_wait(p):
        src = (x + nc - p) % nc
        rcopy(dg.at[src], dg.at[src], x_ss.at[5, p], x_rs.at[5, p], xrow(p), c).wait_recv()

    def x_send(j, val):
        xg[j, x] = val
        over(nc, lambda p: x_copy(j, p).start())

    def early_sends():
        for name in ("top", "d", "td"):
            loads[name].wait()
        x_send(4, topv[...])
        dg[x] = jnp.concatenate([dv[4], dv[3], dv[2], dv[1]], axis=0).astype(BF)
        over(nc, lambda p: d_copy(p).start())

    out_row = lax.broadcasted_iota(jnp.int32, (2 * half, w), 0)
    want = out_row // dc % ny * (nx * dc) + x * (2 * dc) + out_row // half * dc + out_row % dc
    pick = jnp.where(lax.broadcasted_iota(jnp.int32, (2 * half, w), 1) == want, 1.0, 0.0).astype(BF)

    def sel(v):
        return mm_t(pick, v).astype(BF)

    def panels():
        for name in ("l3", "l2", "l1", "l0"):
            loads[name].wait()
        for j in range(SUP):
            for q in range(nc):
                r = y * nx + q * 2 + co
                on = pat[j, c * (ny * nx) + r].astype(F32)
                rows = mv[j, pl.ds(pl.multiple_of(r * pe, pe), pe), :].astype(F32)
                ma[tri(j, j), q * pe:(q + 1) * pe] = (rows * on).astype(BF)
        for k in (2, 1, 0):
            stack = jnp.concatenate([ma[tri(j, k + 1)] for j in range(k + 1, SUP)], axis=0)
            res = mm(stack, lv[k]).astype(BF)
            for i, j in enumerate(range(k + 1, SUP)):
                ma[tri(j, k)] = res[ku * i:ku * (i + 1)]

    def panels_t():
        for j in range(SUP):
            for k in range(j + 1):
                mat[tri(j, k)] = sel(ma[tri(j, k)])

    def d_terms():
        over(nc, d_wait)
        nd = nc * dc
        mrow = lax.broadcasted_iota(jnp.int32, (nd, w), 0)
        at = y * (nx * dc) + mrow // dc * (2 * dc) + co * dc + mrow % dc
        one = jnp.where(lax.broadcasted_iota(jnp.int32, (nd, w), 1) == at, 1.0, 0.0).astype(BF)
        count = jnp.where(c == 0, 1.0, 0.0).astype(F32)
        right, left = [], []
        for k in (3, 2, 1, 0):
            mine = jnp.concatenate([dg[q, (3 - k) * dc:(4 - k) * dc] for q in range(nc)], axis=0)
            right, left = right + [mine], left + [one]
            res = mm(jnp.concatenate(right + left, axis=0), lv[k]).astype(BF)
            n = len(right)
            right = [res[nd * i:nd * (i + 1)] for i in range(n)]
            left = [res[nd * (n + i):nd * (n + i + 1)] for i in range(n)]
            accp[k] = count * mm(sel(res[nd * n:]), res[:nd * n])

    def event(j):
        over(nc, lambda p: x_wait(j, p))
        first_rows = xg[j].reshape(ku, w)
        cur = first_rows
        for k in range(j, -1, -1):
            if k < j:
                cur = mm(cur, lv[k]).astype(BF)
            if k < 4:
                add = None
                if j < 4:
                    add = -mm(mat[tri(j, k)], cur)
                if k < j:
                    more = mm(sel(cur), ma[tri(j - 1, k)])
                    add = more if add is None else add + more
                accp[k] += add
        if j > 0:
            accs[j - 1] = mm(sel(first_rows), ma[tri(j - 1, j - 1)])

    def span(j):
        return (1 if j == 4 else 0), (1 if j == 0 else 2)

    def mats(j):
        out = []
        if j < 4:
            out.append((0, accp.at[j]))
        if j > 0:
            out.append((1, accs.at[j - 1]))
        return out

    def c_copy(j):
        a, b = span(j)
        return rcopy(cs.at[j, a:b], cr.at[j, a:b], c_ss.at[j], c_rs.at[j], twin, c)

    def c_send(j):
        for i, ref in mats(j):
            cs[j, i] = ref[pl.ds(pl.multiple_of((1 - co) * half, half), half), :].astype(BF)
        c_copy(j).start()

    def y_copy(j, p):
        a, b = span(j)
        return rcopy(ys.at[j, (y + p) % ny, a:b], yr.at[j, y, a:b], y_ss.at[j, p], y_rs.at[j, p], yrow(p), c)

    def y_wait(j, p):
        a, b = span(j)
        src = (y + ny - p) % ny
        rcopy(ys.at[j, src, a:b], yr.at[j, src, a:b], y_ss.at[j, p], y_rs.at[j, p], yrow(p), c).wait_recv()

    def y_send(j):
        c_copy(j).wait_recv()
        for i, ref in mats(j):
            tot = ref[pl.ds(pl.multiple_of(co * half, half), half), :] + cr[j, i].astype(F32)
            tot = tot.reshape(ny, dc, w)
            tot = jnp.concatenate([tot[:, :, :w // 2], tot[:, :, w // 2:]], axis=1)
            ys[j, :, i] = tot.astype(BF)
        over(ny, lambda p: y_copy(j, p).start())
        for i, _ in mats(j):
            yr[j, y, i] = ys[j, y, i]

    def f_copy(k):
        return rcopy(fs.at[k], fr.at[c], f_ss.at[k], f_rs.at[c], row, plane_s(k, nz))

    def w_copy(k):
        return rcopy(fw.at[k], fv.at[c], w_ss.at[k], w_rs.at[c], row, plane_w(k, nz))

    def z_send(j):
        over(ny, lambda p: y_wait(j, p))
        for i, _ in mats(j):
            tot = yr[j, 0, i].astype(F32)
            for q in range(1, ny):
                tot = tot + yr[j, q, i].astype(F32)
            if i == 0:
                fw[j] = tot.astype(BF)
            else:
                fs[j - 1] = tot.astype(BF)
        if j < 4:
            @pl.when(c != plane_w(j, nz))
            def _():
                w_copy(j).start()

            @pl.when(c == plane_w(j, nz))
            def _():
                fv[c] = fw[j]
        if j > 0:
            @pl.when(c != plane_s(j - 1, nz))
            def _():
                f_copy(j - 1).start()

            @pl.when(c == plane_s(j - 1, nz))
            def _():
                fr[c] = fs[j - 1]

    def product(k):
        out = pv[k, c]
        for d in range(2):
            h = hops(k, d)
            if h > 0:
                rs_copy(k, d, h - 1).wait_recv()
                out = out + rsr[k, d, h - 1].astype(F32)
        return out

    def finish(k, carried):
        own_mask = pat[k, c * (ny * nx) + row].astype(F32)
        new = (-(product(k) + carried) * own_mask).astype(BF)
        nout[k] = new
        x_send(k, new)
        return new

    def carry():
        return mm(topv[...], lv[3])

    def early4():
        event(4)
        c_send(4)

    hooks = {0: [early_sends], 1: [panels], 2: [d_terms], 3: [early4], 4: [panels_t, lambda: y_send(4)], 5: []}
    state = {}
    for t in range(max(hi, 6)):
        for k in (3, 2, 1, 0):
            if t == OFF[k]:
                product_part(k)
                rs_step(k, 0, 0)
                rs_step(k, 1, 0)
        for k in (3, 2, 1, 0):
            s = t - OFF[k]
            for d in range(2):
                if 0 < s < hops(k, d):
                    rs_step(k, d, s)
        for f in hooks.get(t, ()):
            f()
    b43 = carry()
    z_send(4)
    n3 = finish(3, b43)
    n2 = finish(2, mm(n3, lv[2]))
    n1 = finish(1, mm(n2, lv[1]))
    finish(0, mm(n1, lv[0]))
    out_n = pltpu.make_async_copy(nout, cols_h, out_sem.at[0])
    out_n.start()
    event(3)
    c_send(3)
    event(2)
    c_send(2)
    y_send(3)
    event(1)
    c_send(1)
    y_send(2)
    event(0)
    c_send(0)
    y_send(1)
    y_send(0)
    for s in range(hi):
        for k in range(SUP):
            for d in range(2):
                if s < hops(k, d):
                    rs_copy(k, d, s).wait_send()
    z_send(3)
    z_send(2)
    z_send(1)
    z_send(0)

    def from_plane(p):
        return (c + nz - p) % nz

    def g_copy(k, p):
        return rcopy(gs, ags.at[k], g_ss.at[p], g_rs.at[k], row, (c + p) % nz)

    def h_copy(k, p):
        return rcopy(gw, agw.at[k], h_ss.at[p], h_rs.at[k], row, (c + p) % nz)

    for k in range(SUP):
        @pl.when(c == plane_s(k, nz))
        def _():
            def f_wait(p):
                src = from_plane(p)
                rcopy(fs.at[k], fr.at[src], f_ss.at[k], f_rs.at[src], row, src).wait_recv()

            over(nz, f_wait)
            gs[...] = jnp.sum(fr[...].astype(F32), axis=0).astype(BF)
            over(nz, lambda p: g_copy(k, p).start())
            ags[k] = gs[...]

    for k in range(SUP):
        @pl.when(c == plane_w(k, nz))
        def _():
            def w_wait(p):
                src = from_plane(p)
                rcopy(fw.at[k], fv.at[src], w_ss.at[k], w_rs.at[src], row, src).wait_recv()

            over(nz, w_wait)
            gw[...] = jnp.sum(fv[...].astype(F32), axis=0).astype(BF)
            over(nz, lambda p: h_copy(k, p).start())
            agw[k] = gw[...]

    def drain_x(p):
        for j in range(5):
            x_copy(j, p).wait_send()
        d_copy(p).wait_send()

    def drain_y(p):
        for j in range(5):
            y_copy(j, p).wait_send()

    over(nc, drain_x)
    over(ny, drain_y)
    for j in range(5):
        c_copy(j).wait_send()

    for k in range(SUP):
        @pl.when(c != plane_s(k, nz))
        def _():
            f_copy(k).wait_send()
            g_copy(k, 1).wait_recv()

        @pl.when(c != plane_w(k, nz))
        def _():
            w_copy(k).wait_send()

    for k in (3, 2, 1, 0):
        @pl.when(c != plane_w(k, nz))
        def _():
            h_copy(k, 1).wait_recv()

        dout[k] = dv[k] + unfold(agw[k].astype(F32))
    for k in range(SUP):
        prev = dout[k + 1] if k < 3 else dv[4]
        big = prev.astype(BF)
        small = (prev - big.astype(F32)).astype(BF)
        both = mm(jnp.concatenate([big, small], axis=0), lv[k])
        sout[k] = -(unfold(ags[k].astype(F32)) + both[:dc] + both[dc:])
    out_d = pltpu.make_async_copy(dout, both_h.at[pl.ds(0, SUP)], out_sem.at[1])
    out_s = pltpu.make_async_copy(sout, both_h.at[pl.ds(SUP, SUP)], out_sem.at[2])
    out_d.start()
    out_s.start()

    for k in range(SUP):
        @pl.when(c == plane_w(k, nz))
        def _():
            over(nz, lambda p: h_copy(k, p).wait_send())

    for k in range(SUP):
        @pl.when(c == plane_s(k, nz))
        def _():
            over(nz, lambda p: g_copy(k, p).wait_send())

    out_n.wait()
    out_d.wait()
    out_s.wait()


def local(known_inverse, lower_panel, chain_panel, diag_inverse, top_cols, top_diag, pattern):
    nr = lax.axis_size("rows")
    nz = lax.axis_size("cols")
    nx = 8 if nr >= 64 else 4
    ny = nr // nx
    pe = known_inverse.shape[2]
    w = lower_panel.shape[-1]
    dc = w // nr
    ub = nr * pe
    nc = nx // 2
    hi = nz // 2
    g = known_inverse.reshape(nz * pe, ub)
    m = lower_panel.reshape(SUP, ub, w)
    top = top_cols.reshape(pe, w)
    ku = nc * pe
    half = ny * dc
    dma = pltpu.SemaphoreType.DMA
    vm = pltpu.VMEM
    any_spec = pl.BlockSpec(memory_space=pltpu.HBM)
    scratch = [
        vm((nz * pe, ub), BF), vm((SUP, ub, w), BF), vm((SUP, w, w), BF), vm((SUP + 1, dc, w), F32),
        vm((pe, w), BF), vm((SUP, ub), F32), vm((SUP, nz, pe, w), F32),
        vm((SUP, 2, hi, pe, w), BF), vm((SUP, 2, hi, pe, w), BF),
        vm((5, nc, pe, w), BF), vm((nc, 4 * dc, w), BF), vm((10, ku, w), BF), vm((10, 2 * half, ku), BF),
        vm((SUP, 2 * half, w), F32), vm((SUP, 2 * half, w), F32),
        vm((5, 2, half, w), BF), vm((5, 2, half, w), BF),
        vm((5, ny, 2, 2 * dc, w // 2), BF), vm((5, ny, 2, 2 * dc, w // 2), BF),
        vm((SUP, 2 * dc, w // 2), BF), vm((nz, 2 * dc, w // 2), BF),
        vm((SUP, 2 * dc, w // 2), BF), vm((nz, 2 * dc, w // 2), BF),
        vm((2 * dc, w // 2), BF), vm((2 * dc, w // 2), BF),
        vm((SUP, 2 * dc, w // 2), BF), vm((SUP, 2 * dc, w // 2), BF),
        vm((SUP, pe, w), BF), vm((SUP, dc, w), F32), vm((SUP, dc, w), F32),
        dma((13,)), dma((3,)), dma((SUP, 2, hi)), dma((SUP, 2, hi)),
        dma((6, nc)), dma((6, nc)), dma((5,)), dma((5,)), dma((5, ny)), dma((5, ny)),
        dma((SUP,)), dma((nz,)), dma((SUP,)), dma((nz,)), dma((nz,)), dma((SUP,)), dma((nz,)), dma((SUP,)),
    ]
    cols, both = pl.pallas_call(
        functools.partial(kernel, nz, ny, nx),
        out_shape=(
            jax.ShapeDtypeStruct((SUP, pe, w), BF),
            jax.ShapeDtypeStruct((2 * SUP, dc, w), F32),
        ),
        in_specs=[any_spec] * 6 + [pl.BlockSpec(memory_space=pltpu.SMEM)],
        out_specs=(any_spec,) * 2,
        scratch_shapes=scratch,
        compiler_params=pltpu.CompilerParams(
            collective_id=0, has_side_effects=True, vmem_limit_bytes=64 * 1024 * 1024
        ),
        name="chain",
    )(g, m, chain_panel, diag_inverse, top, top_diag, pattern)
    diag, sub = both[:SUP], both[SUP:]
    return cols.reshape(SUP, 1, 1, pe, w), diag, sub


def solution(mesh):
    in_specs = (
        P(None, "rows", None, "cols"),
        P(None, "cols", None, None, None),
        P(),
        P(None, "rows", None),
        P("cols", "rows", None, None),
        P("rows", None),
        P(),
    )
    out_specs = (P(None, "cols", "rows", None, None), P(None, "rows", None), P(None, "rows", None))
    return jax.shard_map(local, mesh=mesh, in_specs=in_specs, out_specs=out_specs, check_vma=False)
```

time: 98.5 us -> 82.1 us (0.83)
  Pallas kernels: 93.1 us -> 77.6 us
  local copies, waits for them, and re-layouts: 4.51 us -> 3.1 us
    pallas_call x1, Pallas kernels: 93.1 us -> 77.6 us  [local(): pl.pallas_call(functools.partial(kernel, nz, ny, nx), out_shape=(jax.Shap...]
    unnamed x3 -> x1, local copies, waits for them, and re-layouts: 4.51 us -> 1.57 us
    slice x0 -> x1, local copies, waits for them, and re-layouts: none -> 1.53 us  [local(): diag, sub = (both[:SUP], both[SUP:])]
where the time goes in v3:
time: 82.1 us; the launch traced here: 81.4 us
  Pallas kernels  77.6 us (95%)
  local copies, waits for them, and re-layouts  3.1 us (4%)
    pallas_call x1, Pallas kernels, local(): pl.pallas_call(functools.partial(kernel, nz, ny, nx), out_shape=(jax.Shap...  77.6 us

profile of v3, /device:TPU:1, one launch (start us, length us, event | category | flops | bytes accessed | tf_op | source)
XLA Modules:
  0.0 81.4 jit_solution(18024589169719989991)
XLA Ops:
  0.6 77.6 %chain.1 = (bf16[4,32,512]{2,1,0:T(8,128)(2,1)}, f32[8,8,512]{2,1,0:T(8,128)}) custom-call(bf16[384,2048]{1,0:T(8,128)(2,1)} %bitcast.7, bf16[4,2048,512]{2,1,0:T(8,128)(2,1)} %bitcast.6, bf16[4,512,512]{2,1,0:T(8,128)(2,1)} %l_h.1, f32[4,8,512]{2,1,0:T(8,128)} %d_h.1, bf16[32,512]{1,0:T(8,128)(2,1)} %bitcast.9, f32[8,512]{1,0:T(8,128)} %td_h.1, s32[4,768]{1,0:T(4,128)} %pat.1), custom_call_target="tpu_custom_call" | custom-call | tf_op jit(solution)/shard_map/chain/pallas_call | solution.py:502
  78.3 1.5 %fusion = (f32[4,8,512]{2,1,0:T(8,128)}, f32[4,8,512]{2,1,0:T(8,128)}) fusion(f32[8,8,512]{2,1,0:T(8,128)} %get-tuple-element.6), kind=kLoop, calls=%fused_computation | loop fusion | bytes 262144 | tf_op jit(solution)/shard_map/slice | solution.py:516
  79.8 1.6 %copy.12 = bf16[4,1,1,32,512]{4,3,2,1,0:T(8,128)(2,1)} copy(bf16[4,1,1,32,512]{4,3,2,1,0:T(8,128)(2,1)} %bitcast.8) | data formatting | bytes 262144

commit v4 on v3

--- a/solution.py
+++ b/solution.py
@@ -11,7 +11,7 @@
 F32 = jnp.float32
 MESH = pl.DeviceIdType.MESH
 SUP = 4
-OFF = {3: 0, 2: 0, 1: 0, 0: 0}
+OFF = {3: 0, 2: 0, 1: 1, 0: 1}
 
 
 def mm(a, b):
@@ -44,7 +44,7 @@
     return j * (j + 1) // 2 + k
 
 
-def kernel(nz, ny, nx, g_h, m_h, l_h, d_h, top_h, td_h, pat, cols_h, both_h,
+def kernel(nz, ny, nx, g_h, m_h, l_h, d_h, top_h, td_h, pat, cols_h, diag_h, sub_h,
            gv, mv, lv, dv, topv, mlv, pv, rss, rsr, xg, dg, ma, mat, accp, accs, cs, cr, ys, yr,
            fs, fr, fw, fv, gs, gw, ags, agw, nout, dout, sout,
            in_sem, out_sem, rs_ss, rs_rs, x_ss, x_rs, c_ss, c_rs, y_ss, y_rs,
@@ -73,6 +73,7 @@
         loads["l%d" % k] = load(9 + k, l_h.at[k], lv.at[k])
     loads["g"].start()
     loads["m3"].start()
+    loads["m2"].start()
 
     def rcopy(src, dst, ss, rs, trow, tcol):
         return pltpu.make_async_remote_copy(src_ref=src, dst_ref=dst, send_sem=ss, recv_sem=rs,
@@ -114,7 +115,6 @@
 
     lax.fori_loop(0, ny * nx * pe // 128, mask_lanes, 0)
     loads["g"].wait()
-    pl.semaphore_wait(bar, nc + (ny - 1) + (nz - 1))
 
     hi, lo = nz // 2, (nz - 1) // 2
 
@@ -144,7 +144,7 @@
         lhs = gv[...] * mlv[k:k + 1, :].astype(BF)
         pv[k] = mm(lhs, mv[k]).reshape(nz, pe, w)
 
-    after = {3: ("m2", "top", "l3", "l2"), 2: ("m1", "l1", "l0"), 1: ("m0", "d", "td"), 0: ()}
+    after = {3: ("m1",), 2: ("m0", "top", "d", "td", "l3", "l2", "l1", "l0"), 1: (), 0: ()}
 
     def x_copy(j, p):
         return rcopy(xg.at[j, x], xg.at[j, x], x_ss.at[j, p], x_rs.at[j, p], xrow(p), c)
@@ -322,21 +322,29 @@
         x_send(k, new)
         return new
 
-    def carry():
-        return mm(topv[...], lv[3])
-
     def early4():
         event(4)
         c_send(4)
 
-    hooks = {0: [early_sends], 1: [panels], 2: [d_terms], 3: [early4], 4: [panels_t, lambda: y_send(4)], 5: []}
-    state = {}
-    for t in range(max(hi, 6)):
-        for k in (3, 2, 1, 0):
-            if t == OFF[k]:
+    chain = {}
+
+    def upper():
+        chain[3] = finish(3, mm(topv[...], lv[3]))
+        chain[2] = finish(2, mm(chain[3], lv[2]))
+        z_send(4)
+
+    hooks = {1: [early_sends], 2: [panels], 3: [d_terms], 4: [early4], 5: [panels_t, lambda: y_send(4)], 6: [upper]}
+    for t in range(max(hi + 1, 7)):
+        fresh = [k for k in (3, 2, 1, 0) if t == OFF[k]]
+        if t == 0:
+            for k in fresh:
                 product_part(k)
-                rs_step(k, 0, 0)
-                rs_step(k, 1, 0)
+            pl.semaphore_wait(bar, nc + (ny - 1) + (nz - 1))
+        for k in fresh:
+            if t > 0:
+                product_part(k)
+            rs_step(k, 0, 0)
+            rs_step(k, 1, 0)
         for k in (3, 2, 1, 0):
             s = t - OFF[k]
             for d in range(2):
@@ -344,11 +352,7 @@
                     rs_step(k, d, s)
         for f in hooks.get(t, ()):
             f()
-    b43 = carry()
-    z_send(4)
-    n3 = finish(3, b43)
-    n2 = finish(2, mm(n3, lv[2]))
-    n1 = finish(1, mm(n2, lv[1]))
+    n1 = finish(1, mm(chain[2], lv[1]))
     finish(0, mm(n1, lv[0]))
     out_n = pltpu.make_async_copy(nout, cols_h, out_sem.at[0])
     out_n.start()
@@ -431,22 +435,28 @@
         def _():
             w_copy(k).wait_send()
 
+    def take_p(k):
+        @pl.when(c != plane_w(k, nz))
+        def _():
+            h_copy(k, 1).wait_recv()
+
+        dout[k] = dv[k] + unfold(agw[k].astype(F32))
+
     for k in (3, 2, 1, 0):
-        @pl.when(c != plane_w(k, nz))
-        def _():
-            h_copy(k, 1).wait_recv()
-
-        dout[k] = dv[k] + unfold(agw[k].astype(F32))
-    for k in range(SUP):
+        if k < 3:
+            take_p(k + 1)
         prev = dout[k + 1] if k < 3 else dv[4]
         big = prev.astype(BF)
         small = (prev - big.astype(F32)).astype(BF)
         both = mm(jnp.concatenate([big, small], axis=0), lv[k])
         sout[k] = -(unfold(ags[k].astype(F32)) + both[:dc] + both[dc:])
-    out_d = pltpu.make_async_copy(dout, both_h.at[pl.ds(0, SUP)], out_sem.at[1])
-    out_s = pltpu.make_async_copy(sout, both_h.at[pl.ds(SUP, SUP)], out_sem.at[2])
+    out_s = pltpu.make_async_copy(sout, sub_h, out_sem.at[2])
+    out_d = pltpu.make_async_copy(dout.at[1:SUP], diag_h.at[1:SUP], out_sem.at[1])
+    out_s.start()
     out_d.start()
-    out_s.start()
+    take_p(0)
+    out_z = pltpu.make_async_copy(dout.at[0], diag_h.at[0], out_sem.at[3])
+    out_z.start()
 
     for k in range(SUP):
         @pl.when(c == plane_w(k, nz))
@@ -461,6 +471,20 @@
     out_n.wait()
     out_d.wait()
     out_s.wait()
+    out_z.wait()
+
+
+def hand_over(a, b, d, a_out, b_out, d_out, a_v, b_v, d_v, sem, sem_out):
+    trips = ((a, a_v, a_out), (b, b_v, b_out), (d, d_v, d_out))
+    loads = [pltpu.make_async_copy(src, mid, sem.at[i]) for i, (src, mid, _) in enumerate(trips)]
+    stores = [pltpu.make_async_copy(mid, dst, sem_out.at[i]) for i, (_, mid, dst) in enumerate(trips)]
+    for load in loads:
+        load.start()
+    for load, store in zip(loads, stores):
+        load.wait()
+        store.start()
+    for store in stores:
+        store.wait()
 
 
 def local(known_inverse, lower_panel, chain_panel, diag_inverse, top_cols, top_diag, pattern):
@@ -495,25 +519,33 @@
         vm((2 * dc, w // 2), BF), vm((2 * dc, w // 2), BF),
         vm((SUP, 2 * dc, w // 2), BF), vm((SUP, 2 * dc, w // 2), BF),
         vm((SUP, pe, w), BF), vm((SUP, dc, w), F32), vm((SUP, dc, w), F32),
-        dma((13,)), dma((3,)), dma((SUP, 2, hi)), dma((SUP, 2, hi)),
+        dma((13,)), dma((4,)), dma((SUP, 2, hi)), dma((SUP, 2, hi)),
         dma((6, nc)), dma((6, nc)), dma((5,)), dma((5,)), dma((5, ny)), dma((5, ny)),
         dma((SUP,)), dma((nz,)), dma((SUP,)), dma((nz,)), dma((nz,)), dma((SUP,)), dma((nz,)), dma((SUP,)),
     ]
-    cols, both = pl.pallas_call(
+    outs = pl.pallas_call(
         functools.partial(kernel, nz, ny, nx),
         out_shape=(
             jax.ShapeDtypeStruct((SUP, pe, w), BF),
-            jax.ShapeDtypeStruct((2 * SUP, dc, w), F32),
+            jax.ShapeDtypeStruct((SUP, dc, w), F32),
+            jax.ShapeDtypeStruct((SUP, dc, w), F32),
         ),
         in_specs=[any_spec] * 6 + [pl.BlockSpec(memory_space=pltpu.SMEM)],
-        out_specs=(any_spec,) * 2,
+        out_specs=(any_spec,) * 3,
         scratch_shapes=scratch,
         compiler_params=pltpu.CompilerParams(
             collective_id=0, has_side_effects=True, vmem_limit_bytes=64 * 1024 * 1024
         ),
         name="chain",
     )(g, m, chain_panel, diag_inverse, top, top_diag, pattern)
-    diag, sub = both[:SUP], both[SUP:]
+    cols, diag, sub = pl.pallas_call(
+        hand_over,
+        out_shape=tuple(jax.ShapeDtypeStruct(o.shape, o.dtype) for o in outs),
+        in_specs=[any_spec] * 3,
+        out_specs=(any_spec,) * 3,
+        scratch_shapes=[vm(o.shape, o.dtype) for o in outs] + [dma((3,)), dma((3,))],
+        name="hand_over",
+    )(*outs)
     return cols.reshape(SUP, 1, 1, pe, w), diag, sub
 
 

time: 82.1 us -> 78.8 us (0.960)
  local copies, waits for them, and re-layouts: 3.1 us -> 0 us
    pallas_call x1, Pallas kernels: 77.6 us -> 75.3 us  [local(): pl.pallas_call(functools.partial(kernel, nz, ny, nx), out_shape=(jax.Shap...]
    pallas_call x0 -> x1, Pallas kernels: none -> 1.65 us  [local(): pl.pallas_call(hand_over, out_shape=tuple((jax.ShapeDtypeStruct(o.shape,...]
    unnamed x1 -> x0, local copies, waits for them, and re-layouts: 1.57 us -> none
    slice x1 -> x0, local copies, waits for them, and re-layouts: 1.53 us -> none  [local(): diag, sub = (both[:SUP], both[SUP:])]
where the time goes in v4:
time: 78.8 us; the launch traced here: 77.6 us
  Pallas kernels  77 us (98%)
    pallas_call x1, Pallas kernels, local(): pl.pallas_call(functools.partial(kernel, nz, ny, nx), out_shape=(jax.Shap...  75.3 us
    pallas_call x1, Pallas kernels, local(): pl.pallas_call(hand_over, out_shape=tuple((jax.ShapeDtypeStruct(o.shape,...  1.65 us

profile of v4, /device:TPU:1, one launch (start us, length us, event | category | flops | bytes accessed | tf_op | source)
XLA Modules:
  0.0 77.6 jit_solution(15155463136151843122)
XLA Ops:
  0.6 75.3 %chain.1 = (bf16[4,32,512]{2,1,0:T(8,128)(2,1)}, f32[4,8,512]{2,1,0:T(8,128)}, f32[4,8,512]{2,1,0:T(8,128)}) custom-call(bf16[384,2048]{1,0:T(8,128)(2,1)} %bitcast.7, bf16[4,2048,512]{2,1,0:T(8,128)(2,1)} %bitcast.6, bf16[4,512,512]{2,1,0:T(8,128)(2,1)} %l_h.1, f32[4,8,512]{2,1,0:T(8,128)} %d_h.1, bf16[32,512]{1,0:T(8,128)(2,1)} %bitcast.8, f32[8,512]{1,0:T(8,128)} %td_h.1, ...), custom_call_target="tpu_custom_call" | custom-call | tf_op jit(solution)/shard_map/chain/pallas_call | solution.py:526
  76.0 1.6 %hand_over.1 = (bf16[4,32,512]{2,1,0:T(8,128)(2,1)}, f32[4,8,512]{2,1,0:T(8,128)}, f32[4,8,512]{2,1,0:T(8,128)}) custom-call(bf16[4,32,512]{2,1,0:T(8,128)(2,1)} %get-tuple-element.9.a, f32[4,8,512]{2,1,0:T(8,128)} %get-tuple-element.10.b, f32[4,8,512]{2,1,0:T(8,128)} %get-tuple-element.11.d), custom_call_target="tpu_custom_call" | custom-call | tf_op jit(solution)/shard_map/hand_over/pallas_call | solution.py:541

commit v5 on v4

--- a/solution.py
+++ b/solution.py
@@ -11,7 +11,7 @@
 F32 = jnp.float32
 MESH = pl.DeviceIdType.MESH
 SUP = 4
-OFF = {3: 0, 2: 0, 1: 1, 0: 1}
+OFF = {3: 0, 2: 0, 1: 0, 0: 0}
 
 
 def mm(a, b):
@@ -93,10 +93,8 @@
         pl.semaphore_signal(bar, inc=1, device_id=(trow, tcol), device_id_type=MESH)
 
     def over(n, f):
-        def body(p, carry):
+        for p in sorted(range(1, n), key=lambda p: -min(p, n - p)):
             f(p)
-            return carry
-        lax.fori_loop(1, n, body, 0)
 
     over(nc, lambda p: sig(xrow(p), c))
     sig(twin, c)
@@ -337,11 +335,11 @@
     for t in range(max(hi + 1, 7)):
         fresh = [k for k in (3, 2, 1, 0) if t == OFF[k]]
         if t == 0:
-            for k in fresh:
+            for k in (3, 2):
                 product_part(k)
             pl.semaphore_wait(bar, nc + (ny - 1) + (nz - 1))
         for k in fresh:
-            if t > 0:
+            if k < 2:
                 product_part(k)
             rs_step(k, 0, 0)
             rs_step(k, 1, 0)

time: 78.8 us -> 75.7 us (0.961)
  Pallas kernels: 77 us -> 73.7 us
    pallas_call x1, Pallas kernels: 75.3 us -> 72.1 us  [local(): pl.pallas_call(functools.partial(kernel, nz, ny, nx), out_shape=(jax.Shap...]
where the time goes in v5:
time: 75.7 us; the launch traced here: 74.4 us
  Pallas kernels  73.7 us (97%)
    pallas_call x1, Pallas kernels, local(): pl.pallas_call(functools.partial(kernel, nz, ny, nx), out_shape=(jax.Shap...  72.1 us
    pallas_call x1, Pallas kernels, local(): pl.pallas_call(hand_over, out_shape=tuple((jax.ShapeDtypeStruct(o.shape,...  1.65 us

profile of v5, /device:TPU:1, one launch (start us, length us, event | category | flops | bytes accessed | tf_op | source)
XLA Modules:
  0.0 74.4 jit_solution(8036285854184389018)
XLA Ops:
  0.6 72.1 %chain.1 = (bf16[4,32,512]{2,1,0:T(8,128)(2,1)}, f32[4,8,512]{2,1,0:T(8,128)}, f32[4,8,512]{2,1,0:T(8,128)}) custom-call(bf16[384,2048]{1,0:T(8,128)(2,1)} %bitcast.7, bf16[4,2048,512]{2,1,0:T(8,128)(2,1)} %bitcast.6, bf16[4,512,512]{2,1,0:T(8,128)(2,1)} %l_h.1, f32[4,8,512]{2,1,0:T(8,128)} %d_h.1, bf16[32,512]{1,0:T(8,128)(2,1)} %bitcast.8, f32[8,512]{1,0:T(8,128)} %td_h.1, ...), custom_call_target="tpu_custom_call" | custom-call | tf_op jit(solution)/shard_map/chain/pallas_call | solution.py:524
  72.7 1.6 %hand_over.1 = (bf16[4,32,512]{2,1,0:T(8,128)(2,1)}, f32[4,8,512]{2,1,0:T(8,128)}, f32[4,8,512]{2,1,0:T(8,128)}) custom-call(bf16[4,32,512]{2,1,0:T(8,128)(2,1)} %get-tuple-element.9.a, f32[4,8,512]{2,1,0:T(8,128)} %get-tuple-element.10.b, f32[4,8,512]{2,1,0:T(8,128)} %get-tuple-element.11.d), custom_call_target="tpu_custom_call" | custom-call | tf_op jit(solution)/shard_map/hand_over/pallas_call | solution.py:539
